TPU v7x, 256 devices: a whole 4x4x8 slice. The times are simulated.
256 devices in a mesh: rhs: 32 (over x, z_lo, y), node: 8 (over z_hi, core).
Axes of the slice: x: 4, y: 4, z: 8 (z_hi: 4, z_lo: 2; z = z_hi * 2 + z_lo), core: 2. Of those that a mesh axis runs over, the one named last changes fastest.
Arguments:
- right_side: float32 [8192, 8192], P('node', 'rhs'), may hold values from -6 to 6
- diag_inv: float32 [32, 256, 256], P('node', 'rhs'), may hold values from -1 to 1
- lower: float32 [32, 256, 256], P('node', 'rhs'), may hold values from -0.4375 to 0.4375
- factor_pattern: int32 [32, 4, 4], P('node'), may hold values 0 or 1
- jacobian: float32 [32, 256, 768], P('node', 'rhs'), may hold values from -0.078125 to 0.078125
- jacobian_pattern: int32 [32, 4, 12], P('node'), may hold values 0 or 1
Outputs:
- solution: float32 [8192, 8192], P('node', 'rhs')
- residual: float32 [8192, 8192], P('node', 'rhs')
All inputs are finite; a program needn't handle non-finite values. No bound on the sum of `factor_pattern` or of `jacobian_pattern` on one device may be relied on, other than what follows from the above.
Results may differ from a plain program's by a relative error of at most 0.00021.
Values sent between devices are 32-bit elements; how exact they have to be, the bound alone decides.
A program may use at most 64 MiB of HBM per device.

v0:
```python
import jax
import jax.numpy as jnp
from jax import lax
from jax.sharding import PartitionSpec as P

HIGHEST_PREC = lax.Precision.HIGHEST
TRANSPOSED = (((0,), (0,)), ((), ()))


def shifted(value, axis, steps):
    count = lax.axis_size(axis)
    initial, last = (max(0, -steps), min(count, count - steps))
    return lax.ppermute(value, axis, [(source, source + steps) for source in range(initial, last)])


def extended(cells, sides, width):
    for axis, dim in sides:
        count = lax.axis_size(axis)
        ends = count - 1
        head = lax.slice_in_dim(cells, 0, width, axis=dim)
        tail = lax.slice_in_dim(cells, cells.shape[dim] - width, cells.shape[dim], axis=dim)
        cells = jnp.concatenate(
            [
                lax.ppermute(tail, axis, [(i, (i + 1) % count) for i in range(ends)]),
                cells,
                lax.ppermute(head, axis, [((i + 1) % count, i) for i in range(ends)]),
            ],
            axis=dim,
        )
    return cells


def apply_pattern(blocks, pattern):
    supers, row_count, col_count = blocks.shape
    block_size = row_count // pattern.shape[1]
    shaped = blocks.reshape(supers, pattern.shape[1], block_size, pattern.shape[2], block_size)
    weights = pattern.astype(jnp.float32)[:, :, None, :, None]
    return (shaped * weights).reshape(supers, row_count, col_count)


def sweep_down(inverse, masked, rhs_blocks, incoming):

    def advance(previous, inputs):
        inv_block, low_block, rhs_block = inputs
        coupled = jnp.dot(low_block, previous, precision=HIGHEST_PREC)
        solved = jnp.dot(inv_block, rhs_block - coupled, precision=HIGHEST_PREC)
        return (solved, solved)

    outgoing, values = lax.scan(advance, incoming, (inverse, masked, rhs_blocks))
    return (values, outgoing)


def sweep_up(inverse, masked, forward_blocks, incoming):

    def advance(entering, inputs):
        inv_block, low_block, forward_block = inputs
        solved = lax.dot_general(
            inv_block, forward_block - entering, TRANSPOSED, precision=HIGHEST_PREC
        )
        passed = lax.dot_general(low_block, solved, TRANSPOSED, precision=HIGHEST_PREC)
        return (passed, solved)

    outgoing, values = lax.scan(advance, incoming, (inverse, masked, forward_blocks), reverse=True)
    return (values, outgoing)


def jacobian_product(portion, pattern, windows):
    supers, row_count, col_count = portion.shape
    block_count = pattern.shape[1]
    block_size = col_count // pattern.shape[2]
    row_ids = lax.iota(jnp.int32, row_count)
    onehot = (row_ids[:, None] // block_size == lax.iota(jnp.int32, block_count)[None, :]).astype(
        jnp.float32
    )
    weights = jnp.einsum("ra,sac->src", onehot, pattern.astype(jnp.float32))
    shaped = portion.reshape(supers, row_count, pattern.shape[2], block_size)
    masked = (shaped * weights[:, :, :, None]).reshape(supers, row_count, col_count)
    return jnp.einsum("sij,sjr->sir", masked, windows, precision=HIGHEST_PREC)


def on_device(right_side, diag_inv, lower, factor_pattern, jacobian, jacobian_pattern):
    supers = diag_inv.shape[0]
    panel_rows = diag_inv.shape[2]
    columns = right_side.shape[1]
    rhs_blocks = right_side.reshape(supers, panel_rows, columns)
    inverse, lower_all = (
        lax.all_gather(diag_inv, "rhs", axis=1, tiled=True),
        lax.all_gather(lower, "rhs", axis=1, tiled=True),
    )
    masked = apply_pattern(lower_all, factor_pattern)
    zero_state = jnp.zeros((panel_rows, columns), jnp.float32)
    rounds = lax.axis_size("node")

    def relay_down(round_index, incoming):
        unused, outgoing = sweep_down(inverse, masked, rhs_blocks, incoming)
        return shifted(outgoing, "node", 1)

    incoming = lax.fori_loop(0, rounds - 1, relay_down, zero_state)
    forward, unused = sweep_down(inverse, masked, rhs_blocks, incoming)

    def relay_up(round_index, incoming):
        unused, outgoing = sweep_up(inverse, masked, forward, incoming)
        return shifted(outgoing, "node", -1)

    incoming = lax.fori_loop(0, rounds - 1, relay_up, zero_state)
    solution, unused = sweep_up(inverse, masked, forward, incoming)
    span = supers * panel_rows
    flattened = solution.reshape(span, columns)
    padded = extended(flattened, (("node", 0),), panel_rows)
    before = padded[:span].reshape(supers, panel_rows, columns)
    after = padded[2 * panel_rows :].reshape(supers, panel_rows, columns)
    windows = jnp.concatenate([before, solution, after], axis=1)
    product = jacobian_product(
        lax.all_gather(jacobian, "rhs", axis=1, tiled=True), jacobian_pattern, windows
    )
    residual = rhs_blocks - product
    return (flattened, residual.reshape(span, columns))


def solution(mesh):
    in_specs = (
        P("node", "rhs"),
        P("node", "rhs", None),
        P("node", "rhs", None),
        P("node", None, None),
        P("node", "rhs", None),
        P("node", None, None),
    )
    out_specs = (P("node", "rhs"), P("node", "rhs"))
    return jax.shard_map(
        on_device, mesh=mesh, in_specs=in_specs, out_specs=out_specs, check_vma=False
    )
```

profile of v0, /device:TPU:1, one launch (start us, length us, event | category | flops | bytes accessed | tf_op | source)
XLA Modules:
  0.0 639.9 jit_solution(5976639583881987861)
XLA Ops:
  13.5 131.2 %all-gather.4.cloned.1.call-done = f32[4,256,256]{2,1,0:T(8,128)} async-done(((f32[4,8,256]{2,1,0:T(8,128)}), f32[4,256,256]{2,1,0:T(8,128)}) %all-gather.4.cloned.1.call-update) | async-done | bytes 1048592 | tf_op jit(solution)/shard_map/all_gather | solution.py:88
  146.3 153.1 %all-gather.6.cloned.1.call-done = f32[4,256,256]{2,1,0:T(8,128)} async-done(((f32[4,8,256]{2,1,0:T(8,128)}), f32[4,256,256]{2,1,0:T(8,128)}) %all-gather.6.cloned.1.call-update) | async-done | bytes 1048592 | tf_op jit(solution)/shard_map/all_gather | solution.py:87
  299.4 141.4 %while.89 = (s32[]{:T(128)}, f32[256,256]{1,0:T(8,128)S(1)}, f32[4,256,256]{2,1,0:T(8,128)}, f32[4,256,256]{2,1,0:T(8,128)S(1)}, f32[4,256,256]{2,1,0:T(8,128)S(...) while((s32[]{:T(128)}, f32[256,256]{1,0:T(8,128)S(1)}, f32[4,256,256]{2,1,0:T(8,128)}, ...), condition=%wide.region_3.4_spmd, body=%wide.region_0.3_spmd.sunk | while | flops 402718720 | bytes 3409166 | solution.py:98
  299.4 7.0 %while.94 = (s32[]{:T(128)}, f32[256,256]{1,0:T(8,128)S(1)}, f32[4,256,256]{2,1,0:T(8,128)}, f32[4,256,256]{2,1,0:T(8,128)S(1)}, f32[4,256,256]{2,1,0:T(8,128)S(1)}, /*index=5*/s32[]{:T(128)}) while((s32[]{:T(128)}, f32[256,256]{1,0:T(8,128)S(1)}, f32[4,256,256]{2,1,0:T(8,128)}, f32[4,256,256]{2,1,0:T(8,128)S(1)}, ...), condition=%wide.region_2.2_spmd, body=%wide.region_1.1_spmd.sunk | while | flops 402718720 | bytes 1836113 | solution.py:49
  306.4 27.2 %collective-permute-start.1 = (f32[256,256]{1,0:T(8,128)S(1)}, f32[256,256]{1,0:T(8,128)S(1)}, u32[]{:S(2)}, u32[]{:S(2)}) collective-permute-start(f32[256,256]{1,0:T(8,128)S(1)} %get-tuple-element.703), channel_id=1, source_target_pairs={{0,1},{1,2},{2,3},{3,4},{4,5},{5,6},{6,7},{8,9},{9,10},{10,11},{11... | collective-permute-start | bytes 786440 | tf_op jit(solution)/shard_map/while/body/eval_jaxpr/ppermute | solution.py:13
  338.1 7.0 %while.94 = (s32[]{:T(128)}, f32[256,256]{1,0:T(8,128)S(1)}, f32[4,256,256]{2,1,0:T(8,128)}, f32[4,256,256]{2,1,0:T(8,128)S(1)}, f32[4,256,256]{2,1,0:T(8,128)S(1)}, /*index=5*/s32[]{:T(128)}) while((s32[]{:T(128)}, f32[256,256]{1,0:T(8,128)S(1)}, f32[4,256,256]{2,1,0:T(8,128)}, f32[4,256,256]{2,1,0:T(8,128)S(1)}, ...), condition=%wide.region_2.2_spmd, body=%wide.region_1.1_spmd.sunk | while | flops 402718720 | bytes 1836113 | solution.py:49
  354.9 7.0 %while.94 = (s32[]{:T(128)}, f32[256,256]{1,0:T(8,128)S(1)}, f32[4,256,256]{2,1,0:T(8,128)}, f32[4,256,256]{2,1,0:T(8,128)S(1)}, f32[4,256,256]{2,1,0:T(8,128)S(1)}, /*index=5*/s32[]{:T(128)}) while((s32[]{:T(128)}, f32[256,256]{1,0:T(8,128)S(1)}, f32[4,256,256]{2,1,0:T(8,128)}, f32[4,256,256]{2,1,0:T(8,128)S(1)}, ...), condition=%wide.region_2.2_spmd, body=%wide.region_1.1_spmd.sunk | while | flops 402718720 | bytes 1836113 | solution.py:49
  371.0 7.0 %while.94 = (s32[]{:T(128)}, f32[256,256]{1,0:T(8,128)S(1)}, f32[4,256,256]{2,1,0:T(8,128)}, f32[4,256,256]{2,1,0:T(8,128)S(1)}, f32[4,256,256]{2,1,0:T(8,128)S(1)}, /*index=5*/s32[]{:T(128)}) while((s32[]{:T(128)}, f32[256,256]{1,0:T(8,128)S(1)}, f32[4,256,256]{2,1,0:T(8,128)}, f32[4,256,256]{2,1,0:T(8,128)S(1)}, ...), condition=%wide.region_2.2_spmd, body=%wide.region_1.1_spmd.sunk | while | flops 402718720 | bytes 1836113 | solution.py:49
  388.8 7.0 %while.94 = (s32[]{:T(128)}, f32[256,256]{1,0:T(8,128)S(1)}, f32[4,256,256]{2,1,0:T(8,128)}, f32[4,256,256]{2,1,0:T(8,128)S(1)}, f32[4,256,256]{2,1,0:T(8,128)S(1)}, /*index=5*/s32[]{:T(128)}) while((s32[]{:T(128)}, f32[256,256]{1,0:T(8,128)S(1)}, f32[4,256,256]{2,1,0:T(8,128)}, f32[4,256,256]{2,1,0:T(8,128)S(1)}, ...), condition=%wide.region_2.2_spmd, body=%wide.region_1.1_spmd.sunk | while | flops 402718720 | bytes 1836113 | solution.py:49
  404.9 7.0 %while.94 = (s32[]{:T(128)}, f32[256,256]{1,0:T(8,128)S(1)}, f32[4,256,256]{2,1,0:T(8,128)}, f32[4,256,256]{2,1,0:T(8,128)S(1)}, f32[4,256,256]{2,1,0:T(8,128)S(1)}, /*index=5*/s32[]{:T(128)}) while((s32[]{:T(128)}, f32[256,256]{1,0:T(8,128)S(1)}, f32[4,256,256]{2,1,0:T(8,128)}, f32[4,256,256]{2,1,0:T(8,128)S(1)}, ...), condition=%wide.region_2.2_spmd, body=%wide.region_1.1_spmd.sunk | while | flops 402718720 | bytes 1836113 | solution.py:49
  421.6 7.0 %while.94 = (s32[]{:T(128)}, f32[256,256]{1,0:T(8,128)S(1)}, f32[4,256,256]{2,1,0:T(8,128)}, f32[4,256,256]{2,1,0:T(8,128)S(1)}, f32[4,256,256]{2,1,0:T(8,128)S(1)}, /*index=5*/s32[]{:T(128)}) while((s32[]{:T(128)}, f32[256,256]{1,0:T(8,128)S(1)}, f32[4,256,256]{2,1,0:T(8,128)}, f32[4,256,256]{2,1,0:T(8,128)S(1)}, ...), condition=%wide.region_2.2_spmd, body=%wide.region_1.1_spmd.sunk | while | flops 402718720 | bytes 1836113 | solution.py:49
  428.6 7.2 %collective-permute-start.1 = (f32[256,256]{1,0:T(8,128)S(1)}, f32[256,256]{1,0:T(8,128)S(1)}, u32[]{:S(2)}, u32[]{:S(2)}) collective-permute-start(f32[256,256]{1,0:T(8,128)S(1)} %get-tuple-element.703), channel_id=1, source_target_pairs={{0,1},{1,2},{2,3},{3,4},{4,5},{5,6},{6,7},{8,9},{9,10},{10,11},{11... | collective-permute-start | bytes 786440 | tf_op jit(solution)/shard_map/while/body/eval_jaxpr/ppermute | solution.py:13
  440.9 7.0 %while.90 = (s32[]{:T(128)}, f32[256,256]{1,0:T(8,128)S(1)}, f32[4,256,256]{2,1,0:T(8,128)S(1)}, f32[4,256,256]{2,1,0:T(8,128)}, f32[4,256,256]{2,1,0:T(8,128)S(1)}, /*index=5*/f32[4,256,256]{2,1,0:T(8,128)S(1)}, s32[]{:T(128)}) while((s32[]{:T(128)}, f32[256,256]{1,0:T(8,128)S(1)}, f32[4,256,256]{2,1,0:T(8,128)S(1)}, ...), condition=%wide.region_5.6_spmd, body=%wide.region_4.5_spmd.sunk | while | flops 402718720 | bytes 2099285 | solution.py:49
  447.9 138.3 %while.92 = (s32[]{:T(128)}, f32[256,256]{1,0:T(8,128)S(1)}, f32[4,256,256]{2,1,0:T(8,128)S(1)}, f32[4,256,256]{2,1,0:T(8,128)}, f32[4,256,256]{2,1,0:T(8,128)S(...) while((s32[]{:T(128)}, f32[256,256]{1,0:T(8,128)S(1)}, f32[4,256,256]{2,1,0:T(8,128)S(1)}, ...), condition=%wide.region_9.10_spmd, body=%wide.region_6.9_spmd.sunk | while | flops 402718720 | bytes 3409194 | solution.py:105
  447.9 8.7 %while.95 = (s32[]{:T(128)}, f32[256,256]{1,0:T(8,128)S(1)}, f32[4,256,256]{2,1,0:T(8,128)S(1)}, f32[4,256,256]{2,1,0:T(8,128)}, f32[4,256,256]{2,1,0:T(8,128)S(1)}, /*index=5*/s32[]{:T(128)}, s32[]{:T(128)}) while((s32[]{:T(128)}, f32[256,256]{1,0:T(8,128)S(1)}, f32[4,256,256]{2,1,0:T(8,128)S(1)}, f32[4,256,256]{2,1,0:T(8,128)}, ...), condition=%wide.region_8.8_spmd, body=%wide.region_7.7_spmd.sunk | while | flops 402718720 | bytes 1836133 | solution.py:63
  458.6 7.9 %collective-permute-done = f32[256,256]{1,0:T(8,128)} collective-permute-done((f32[256,256]{1,0:T(8,128)S(1)}, f32[256,256]{1,0:T(8,128)}, u32[]{:S(2)}, u32[]{:S(2)}) %collective-permute-start) | collective-permute-done | bytes 262176 | tf_op jit(solution)/shard_map/while/body/eval_jaxpr/ppermute | solution.py:13
  467.4 8.7 %while.95 = (s32[]{:T(128)}, f32[256,256]{1,0:T(8,128)S(1)}, f32[4,256,256]{2,1,0:T(8,128)S(1)}, f32[4,256,256]{2,1,0:T(8,128)}, f32[4,256,256]{2,1,0:T(8,128)S(1)}, /*index=5*/s32[]{:T(128)}, s32[]{:T(128)}) while((s32[]{:T(128)}, f32[256,256]{1,0:T(8,128)S(1)}, f32[4,256,256]{2,1,0:T(8,128)S(1)}, f32[4,256,256]{2,1,0:T(8,128)}, ...), condition=%wide.region_8.8_spmd, body=%wide.region_7.7_spmd.sunk | while | flops 402718720 | bytes 1836133 | solution.py:63
  478.1 8.3 %collective-permute-done = f32[256,256]{1,0:T(8,128)} collective-permute-done((f32[256,256]{1,0:T(8,128)S(1)}, f32[256,256]{1,0:T(8,128)}, u32[]{:S(2)}, u32[]{:S(2)}) %collective-permute-start) | collective-permute-done | bytes 262176 | tf_op jit(solution)/shard_map/while/body/eval_jaxpr/ppermute | solution.py:13
  487.3 8.7 %while.95 = (s32[]{:T(128)}, f32[256,256]{1,0:T(8,128)S(1)}, f32[4,256,256]{2,1,0:T(8,128)S(1)}, f32[4,256,256]{2,1,0:T(8,128)}, f32[4,256,256]{2,1,0:T(8,128)S(1)}, /*index=5*/s32[]{:T(128)}, s32[]{:T(128)}) while((s32[]{:T(128)}, f32[256,256]{1,0:T(8,128)S(1)}, f32[4,256,256]{2,1,0:T(8,128)S(1)}, f32[4,256,256]{2,1,0:T(8,128)}, ...), condition=%wide.region_8.8_spmd, body=%wide.region_7.7_spmd.sunk | while | flops 402718720 | bytes 1836133 | solution.py:63
  497.9 9.0 %collective-permute-done = f32[256,256]{1,0:T(8,128)} collective-permute-done((f32[256,256]{1,0:T(8,128)S(1)}, f32[256,256]{1,0:T(8,128)}, u32[]{:S(2)}, u32[]{:S(2)}) %collective-permute-start) | collective-permute-done | bytes 262176 | tf_op jit(solution)/shard_map/while/body/eval_jaxpr/ppermute | solution.py:13
  507.9 8.7 %while.95 = (s32[]{:T(128)}, f32[256,256]{1,0:T(8,128)S(1)}, f32[4,256,256]{2,1,0:T(8,128)S(1)}, f32[4,256,256]{2,1,0:T(8,128)}, f32[4,256,256]{2,1,0:T(8,128)S(1)}, /*index=5*/s32[]{:T(128)}, s32[]{:T(128)}) while((s32[]{:T(128)}, f32[256,256]{1,0:T(8,128)S(1)}, f32[4,256,256]{2,1,0:T(8,128)S(1)}, f32[4,256,256]{2,1,0:T(8,128)}, ...), condition=%wide.region_8.8_spmd, body=%wide.region_7.7_spmd.sunk | while | flops 402718720 | bytes 1836133 | solution.py:63
  518.5 8.0 %collective-permute-done = f32[256,256]{1,0:T(8,128)} collective-permute-done((f32[256,256]{1,0:T(8,128)S(1)}, f32[256,256]{1,0:T(8,128)}, u32[]{:S(2)}, u32[]{:S(2)}) %collective-permute-start) | collective-permute-done | bytes 262176 | tf_op jit(solution)/shard_map/while/body/eval_jaxpr/ppermute | solution.py:13
  527.5 8.7 %while.95 = (s32[]{:T(128)}, f32[256,256]{1,0:T(8,128)S(1)}, f32[4,256,256]{2,1,0:T(8,128)S(1)}, f32[4,256,256]{2,1,0:T(8,128)}, f32[4,256,256]{2,1,0:T(8,128)S(1)}, /*index=5*/s32[]{:T(128)}, s32[]{:T(128)}) while((s32[]{:T(128)}, f32[256,256]{1,0:T(8,128)S(1)}, f32[4,256,256]{2,1,0:T(8,128)S(1)}, f32[4,256,256]{2,1,0:T(8,128)}, ...), condition=%wide.region_8.8_spmd, body=%wide.region_7.7_spmd.sunk | while | flops 402718720 | bytes 1836133 | solution.py:63
  538.1 8.0 %collective-permute-done = f32[256,256]{1,0:T(8,128)} collective-permute-done((f32[256,256]{1,0:T(8,128)S(1)}, f32[256,256]{1,0:T(8,128)}, u32[]{:S(2)}, u32[]{:S(2)}) %collective-permute-start) | collective-permute-done | bytes 262176 | tf_op jit(solution)/shard_map/while/body/eval_jaxpr/ppermute | solution.py:13
  547.0 8.7 %while.95 = (s32[]{:T(128)}, f32[256,256]{1,0:T(8,128)S(1)}, f32[4,256,256]{2,1,0:T(8,128)S(1)}, f32[4,256,256]{2,1,0:T(8,128)}, f32[4,256,256]{2,1,0:T(8,128)S(1)}, /*index=5*/s32[]{:T(128)}, s32[]{:T(128)}) while((s32[]{:T(128)}, f32[256,256]{1,0:T(8,128)S(1)}, f32[4,256,256]{2,1,0:T(8,128)S(1)}, f32[4,256,256]{2,1,0:T(8,128)}, ...), condition=%wide.region_8.8_spmd, body=%wide.region_7.7_spmd.sunk | while | flops 402718720 | bytes 1836133 | solution.py:63
  557.7 8.0 %collective-permute-done = f32[256,256]{1,0:T(8,128)} collective-permute-done((f32[256,256]{1,0:T(8,128)S(1)}, f32[256,256]{1,0:T(8,128)}, u32[]{:S(2)}, u32[]{:S(2)}) %collective-permute-start) | collective-permute-done | bytes 262176 | tf_op jit(solution)/shard_map/while/body/eval_jaxpr/ppermute | solution.py:13
  566.6 8.7 %while.95 = (s32[]{:T(128)}, f32[256,256]{1,0:T(8,128)S(1)}, f32[4,256,256]{2,1,0:T(8,128)S(1)}, f32[4,256,256]{2,1,0:T(8,128)}, f32[4,256,256]{2,1,0:T(8,128)S(1)}, /*index=5*/s32[]{:T(128)}, s32[]{:T(128)}) while((s32[]{:T(128)}, f32[256,256]{1,0:T(8,128)S(1)}, f32[4,256,256]{2,1,0:T(8,128)S(1)}, f32[4,256,256]{2,1,0:T(8,128)}, ...), condition=%wide.region_8.8_spmd, body=%wide.region_7.7_spmd.sunk | while | flops 402718720 | bytes 1836133 | solution.py:63
  577.3 8.0 %collective-permute-done = f32[256,256]{1,0:T(8,128)} collective-permute-done((f32[256,256]{1,0:T(8,128)S(1)}, f32[256,256]{1,0:T(8,128)}, u32[]{:S(2)}, u32[]{:S(2)}) %collective-permute-start) | collective-permute-done | bytes 262176 | tf_op jit(solution)/shard_map/while/body/eval_jaxpr/ppermute | solution.py:13
  587.3 11.5 %while.93 = (s32[]{:T(128)}, f32[256,256]{1,0:T(8,128)S(1)}, f32[4,256,256]{2,1,0:T(8,128)}, f32[4,256,256]{2,1,0:T(8,128)S(1)}, f32[4,256,256]{2,1,0:T(8,128)},...) while((s32[]{:T(128)}, f32[256,256]{1,0:T(8,128)S(1)}, f32[4,256,256]{2,1,0:T(8,128)}, ...), condition=%wide.region_11.12_spmd, body=%wide.region_10.11_spmd.sunk | while | flops 402718720 | bytes 2098797 | solution.py:63
  599.9 5.7 collective-permute-start.2
  608.9 9.5 %collective-permute-done.3 = f32[256,256]{1,0:T(8,128)S(1)} collective-permute-done((f32[256,256]{1,0:T(8,128)S(1)}, f32[256,256]{1,0:T(8,128)S(1)}, u32[]{:S(2)}, u32[]{:S(2)}) %collective-permute-start.3) | collective-permute-done | bytes 262176 | tf_op jit(solution)/shard_map/ppermute | solution.py:26
  627.1 6.4 fusion.38
  (191 shorter events, 226.5 us)
Async XLA Ops:
  7.2 137.5 %all-gather.4.cloned.1.call-start = ((), (), s32[]{:S(2)}) async-start(), calls=%async_computation | async-start | bytes 1081344 | tf_op jit(solution)/shard_map/all_gather | solution.py:88
  7.9 291.5 %all-gather.6.cloned.1.call-start = ((), (), s32[]{:S(2)}) async-start(), calls=%async_computation.1 | async-start | bytes 1081344 | tf_op jit(solution)/shard_map/all_gather | solution.py:87
  8.6 611.3 %all-gather.8.cloned.1.call-start = ((), (), s32[]{:S(2)}) async-start(), calls=%async_computation.2 | async-start | bytes 3244032 | tf_op jit(solution)/shard_map/all_gather | solution.py:114
  11.3 288.1 %copy-start = (f32[1024,256]{1,0:T(8,128)S(1)}, f32[1024,256]{1,0:T(8,128)}, u32[]{:S(2)}) copy-start(f32[1024,256]{1,0:T(8,128)} %param.18) | copy-start | bytes 3145732
  306.4 31.6 %collective-permute-start.1 = (f32[256,256]{1,0:T(8,128)S(1)}, f32[256,256]{1,0:T(8,128)S(1)}, u32[]{:S(2)}, u32[]{:S(2)}) collective-permute-start(f32[256,256]{1,0:T(8,128)S(1)} %get-tuple-element.703), channel_id=1, source_target_pairs={{0,1},{1,2},{2,3},{3,4},{4,5},{5,6},{6,7},{8,9},{9,10},{10,11},{11... | collective-permute-start | bytes 786440 | tf_op jit(solution)/shard_map/while/body/eval_jaxpr/ppermute | solution.py:13
  345.1 9.8 %collective-permute-start.1 = (f32[256,256]{1,0:T(8,128)S(1)}, f32[256,256]{1,0:T(8,128)S(1)}, u32[]{:S(2)}, u32[]{:S(2)}) collective-permute-start(f32[256,256]{1,0:T(8,128)S(1)} %get-tuple-element.703), channel_id=1, source_target_pairs={{0,1},{1,2},{2,3},{3,4},{4,5},{5,6},{6,7},{8,9},{9,10},{10,11},{11... | collective-permute-start | bytes 786440 | tf_op jit(solution)/shard_map/while/body/eval_jaxpr/ppermute | solution.py:13
  361.8 9.2 %collective-permute-start.1 = (f32[256,256]{1,0:T(8,128)S(1)}, f32[256,256]{1,0:T(8,128)S(1)}, u32[]{:S(2)}, u32[]{:S(2)}) collective-permute-start(f32[256,256]{1,0:T(8,128)S(1)} %get-tuple-element.703), channel_id=1, source_target_pairs={{0,1},{1,2},{2,3},{3,4},{4,5},{5,6},{6,7},{8,9},{9,10},{10,11},{11... | collective-permute-start | bytes 786440 | tf_op jit(solution)/shard_map/while/body/eval_jaxpr/ppermute | solution.py:13
  378.0 10.7 %collective-permute-start.1 = (f32[256,256]{1,0:T(8,128)S(1)}, f32[256,256]{1,0:T(8,128)S(1)}, u32[]{:S(2)}, u32[]{:S(2)}) collective-permute-start(f32[256,256]{1,0:T(8,128)S(1)} %get-tuple-element.703), channel_id=1, source_target_pairs={{0,1},{1,2},{2,3},{3,4},{4,5},{5,6},{6,7},{8,9},{9,10},{10,11},{11... | collective-permute-start | bytes 786440 | tf_op jit(solution)/shard_map/while/body/eval_jaxpr/ppermute | solution.py:13
  395.8 9.1 %collective-permute-start.1 = (f32[256,256]{1,0:T(8,128)S(1)}, f32[256,256]{1,0:T(8,128)S(1)}, u32[]{:S(2)}, u32[]{:S(2)}) collective-permute-start(f32[256,256]{1,0:T(8,128)S(1)} %get-tuple-element.703), channel_id=1, source_target_pairs={{0,1},{1,2},{2,3},{3,4},{4,5},{5,6},{6,7},{8,9},{9,10},{10,11},{11... | collective-permute-start | bytes 786440 | tf_op jit(solution)/shard_map/while/body/eval_jaxpr/ppermute | solution.py:13
  411.9 9.6 %collective-permute-start.1 = (f32[256,256]{1,0:T(8,128)S(1)}, f32[256,256]{1,0:T(8,128)S(1)}, u32[]{:S(2)}, u32[]{:S(2)}) collective-permute-start(f32[256,256]{1,0:T(8,128)S(1)} %get-tuple-element.703), channel_id=1, source_target_pairs={{0,1},{1,2},{2,3},{3,4},{4,5},{5,6},{6,7},{8,9},{9,10},{10,11},{11... | collective-permute-start | bytes 786440 | tf_op jit(solution)/shard_map/while/body/eval_jaxpr/ppermute | solution.py:13
  428.6 12.2 %collective-permute-start.1 = (f32[256,256]{1,0:T(8,128)S(1)}, f32[256,256]{1,0:T(8,128)S(1)}, u32[]{:S(2)}, u32[]{:S(2)}) collective-permute-start(f32[256,256]{1,0:T(8,128)S(1)} %get-tuple-element.703), channel_id=1, source_target_pairs={{0,1},{1,2},{2,3},{3,4},{4,5},{5,6},{6,7},{8,9},{9,10},{10,11},{11... | collective-permute-start | bytes 786440 | tf_op jit(solution)/shard_map/while/body/eval_jaxpr/ppermute | solution.py:13
  456.7 9.8 %collective-permute-start = (f32[256,256]{1,0:T(8,128)S(1)}, f32[256,256]{1,0:T(8,128)}, u32[]{:S(2)}, u32[]{:S(2)}) collective-permute-start(f32[256,256]{1,0:T(8,128)S(1)} %get-tuple-element.718), channel_id=1, source_target_pairs={{1,0},{2,1},{3,2},{4,3},{5,4},{6,5},{7,6},{9,8},{10,9},{11,10},{12... | collective-permute-start | bytes 786440 | tf_op jit(solution)/shard_map/while/body/eval_jaxpr/ppermute | solution.py:13
  476.2 10.2 %collective-permute-start = (f32[256,256]{1,0:T(8,128)S(1)}, f32[256,256]{1,0:T(8,128)}, u32[]{:S(2)}, u32[]{:S(2)}) collective-permute-start(f32[256,256]{1,0:T(8,128)S(1)} %get-tuple-element.718), channel_id=1, source_target_pairs={{1,0},{2,1},{3,2},{4,3},{5,4},{6,5},{7,6},{9,8},{10,9},{11,10},{12... | collective-permute-start | bytes 786440 | tf_op jit(solution)/shard_map/while/body/eval_jaxpr/ppermute | solution.py:13
  496.0 10.9 %collective-permute-start = (f32[256,256]{1,0:T(8,128)S(1)}, f32[256,256]{1,0:T(8,128)}, u32[]{:S(2)}, u32[]{:S(2)}) collective-permute-start(f32[256,256]{1,0:T(8,128)S(1)} %get-tuple-element.718), channel_id=1, source_target_pairs={{1,0},{2,1},{3,2},{4,3},{5,4},{6,5},{7,6},{9,8},{10,9},{11,10},{12... | collective-permute-start | bytes 786440 | tf_op jit(solution)/shard_map/while/body/eval_jaxpr/ppermute | solution.py:13
  516.6 9.9 %collective-permute-start = (f32[256,256]{1,0:T(8,128)S(1)}, f32[256,256]{1,0:T(8,128)}, u32[]{:S(2)}, u32[]{:S(2)}) collective-permute-start(f32[256,256]{1,0:T(8,128)S(1)} %get-tuple-element.718), channel_id=1, source_target_pairs={{1,0},{2,1},{3,2},{4,3},{5,4},{6,5},{7,6},{9,8},{10,9},{11,10},{12... | collective-permute-start | bytes 786440 | tf_op jit(solution)/shard_map/while/body/eval_jaxpr/ppermute | solution.py:13
  536.2 9.9 %collective-permute-start = (f32[256,256]{1,0:T(8,128)S(1)}, f32[256,256]{1,0:T(8,128)}, u32[]{:S(2)}, u32[]{:S(2)}) collective-permute-start(f32[256,256]{1,0:T(8,128)S(1)} %get-tuple-element.718), channel_id=1, source_target_pairs={{1,0},{2,1},{3,2},{4,3},{5,4},{6,5},{7,6},{9,8},{10,9},{11,10},{12... | collective-permute-start | bytes 786440 | tf_op jit(solution)/shard_map/while/body/eval_jaxpr/ppermute | solution.py:13
  555.8 9.9 %collective-permute-start = (f32[256,256]{1,0:T(8,128)S(1)}, f32[256,256]{1,0:T(8,128)}, u32[]{:S(2)}, u32[]{:S(2)}) collective-permute-start(f32[256,256]{1,0:T(8,128)S(1)} %get-tuple-element.718), channel_id=1, source_target_pairs={{1,0},{2,1},{3,2},{4,3},{5,4},{6,5},{7,6},{9,8},{10,9},{11,10},{12... | collective-permute-start | bytes 786440 | tf_op jit(solution)/shard_map/while/body/eval_jaxpr/ppermute | solution.py:13
  575.3 9.9 %collective-permute-start = (f32[256,256]{1,0:T(8,128)S(1)}, f32[256,256]{1,0:T(8,128)}, u32[]{:S(2)}, u32[]{:S(2)}) collective-permute-start(f32[256,256]{1,0:T(8,128)S(1)} %get-tuple-element.718), channel_id=1, source_target_pairs={{1,0},{2,1},{3,2},{4,3},{5,4},{6,5},{7,6},{9,8},{10,9},{11,10},{12... | collective-permute-start | bytes 786440 | tf_op jit(solution)/shard_map/while/body/eval_jaxpr/ppermute | solution.py:13
  587.3 20.5 %copy-start.2 = (s32[4,4,12]{2,1,0:T(4,128)S(1)}, s32[4,4,12]{2,1,0:T(4,128)}, u32[]{:S(2)}) copy-start(s32[4,4,12]{2,1,0:T(4,128)} %param.23) | copy-start | bytes 2308
  599.9 9.1 %collective-permute-start.2 = (f32[256,256]{1,0:T(8,128)S(1)}, f32[256,256]{1,0:T(8,128)S(1)}, u32[]{:S(2)}, u32[]{:S(2)}) collective-permute-start(f32[256,256]{1,0:T(8,128)S(1)} %get-tuple-element.504), channel_id=1, source_target_pairs={{0,1},{1,2},{2,3},{3,4},{4,5},{5,6},{6,7},{8,9},{9,10},{10,11},{11... | collective-permute-start | bytes 786440 | tf_op jit(solution)/shard_map/ppermute | solution.py:24
  605.6 12.8 %collective-permute-start.3 = (f32[256,256]{1,0:T(8,128)S(1)}, f32[256,256]{1,0:T(8,128)S(1)}, u32[]{:S(2)}, u32[]{:S(2)}) collective-permute-start(f32[256,256]{1,0:T(8,128)S(1)} %get-tuple-element.505), channel_id=1, source_target_pairs={{1,0},{2,1},{3,2},{4,3},{5,4},{6,5},{7,6},{9,8},{10,9},{11,10},{12... | collective-permute-start | bytes 786440 | tf_op jit(solution)/shard_map/ppermute | solution.py:26
  624.8 2.2 copy-start.1
Sparse Core Ops, SparseCore 0:
  9.8 134.8 all-gather.3
  146.4 152.9 all-gather.5
  301.2 158.2 all-gather.7
where the time goes:
time: 643 us; the launch traced here: 640 us
  waiting for transfers between devices  384 us (60%)
  matrix products  133 us (21%)
  starting transfers between devices  82.5 us (13%)
  local copies, waits for them, and re-layouts  17.9 us (3%)
  between operations  13.9 us (2%)
    all_gather x1, waiting for transfers between devices, on_device(): lax.all_gather(diag_inv, 'rhs', axis=1, tiled=True)  153 us
    all_gather x1, waiting for transfers between devices, on_device(): lax.all_gather(lower, 'rhs', axis=1, tiled=True)  131 us
    ppermute x14, waiting for transfers between devices, shifted(): lax.ppermute(value, axis, [(source, source + steps) for source in range(i...  88.2 us
    ppermute x14, starting transfers between devices, shifted(): lax.ppermute(value, axis, [(source, source + steps) for source in range(i...  74.5 us
    dot_general x32, matrix products, advance(): lax.dot_general(inv_block, forward_block - entering, TRANSPOSED, precisio...  52.3 us
    dot_general x32, matrix products, advance(): solved = jnp.dot(inv_block, rhs_block - coupled, precision=HIGHEST_PREC)  42.7 us
    dot_general x32, matrix products, advance(): lax.dot_general(low_block, solved, TRANSPOSED, precision=HIGHEST_PREC)  19.3 us
  transfers between devices with their start and end apart: 19, of which 18 were waited for; matrix products, arithmetic and copies ran while one was open for 22% of the time, Pallas kernels for 0%

commit v1 on v0

v1 whole, which is shorter than its diff:
```python
import jax
import jax.numpy as jnp
from jax import lax
from jax.experimental import pallas as pl
from jax.experimental.pallas import tpu as pltpu
from jax.sharding import PartitionSpec as P

MESH_ID = pl.DeviceIdType.MESH
B = 64
W = 256
NODES = 8
HALF = 128


class Sems:
    def __init__(self, send, recv, local):
        self.send, self.recv, self.local = send, recv, local
        self.pairs = self.locals = 0

    def pair(self):
        k = self.pairs
        self.pairs += 1
        return self.send.at[k], self.recv.at[k]

    def one(self):
        k = self.locals
        self.locals += 1
        return self.local.at[k]


class Ring:
    def __init__(self, sems, where, pos, device_at):
        self.where, self.pos = where, pos
        self.up, self.down = device_at(lax.rem(pos + 1, 4)), device_at(lax.rem(pos + 3, 4))
        self.sems = {key: sems.pair() for key in ("u0", "d0", "u1", "d1", "fu", "fd")}
        self.started = []

    def at(self, q, step):
        return self.where(q, lax.rem(self.pos + step, 4))

    def copy(self, key, q, step, device, source=None):
        part = self.at(q, step)
        send, recv = self.sems[key]
        return pltpu.make_async_remote_copy(
            src_ref=part if source is None else source,
            dst_ref=part,
            send_sem=send,
            recv_sem=recv,
            device_id=device,
            device_id_type=MESH_ID,
        )

    def go(self, *args):
        copy = self.copy(*args)
        copy.start()
        self.started.append(copy)

    def direct(self, q, source=None):
        first, second = ("u", "d") if q == 0 else ("d", "u")
        for way in (first, second):
            self.go(f"{way}{q}", q, 0, self.up if way == "u" else self.down, source)

    def forward(self, q):
        if q == 0:
            self.copy("u0", 0, 3, self.up).wait_recv()
            self.go("fu", 0, 3, self.up)
        else:
            self.copy("d1", 1, 1, self.down).wait_recv()
            self.go("fd", 1, 1, self.down)

    def finish(self, q):
        if q == 0:
            self.copy("d0", 0, 1, self.down).wait_recv()
            self.copy("fu", 0, 2, self.up).wait_recv()
        else:
            self.copy("u1", 1, 3, self.up).wait_recv()
            self.copy("fd", 1, 2, self.down).wait_recv()

    def sent(self):
        for copy in self.started:
            copy.wait_send()


class Gather:
    def __init__(self, sems, buf, x, zl, y, device, y_first):
        self.own = buf.at[x, zl, y]

        def layer(q):
            return zl if q == 0 else 1 - zl

        if y_first:
            self.first = Ring(sems, lambda q, p: buf.at[x, layer(q), p], y, lambda p: device(x, zl, p))
            self.second = Ring(sems, lambda q, p: buf.at[p, layer(q)], x, lambda p: device(p, zl, y))
        else:
            self.first = Ring(sems, lambda q, p: buf.at[p, layer(q), y], x, lambda p: device(p, zl, y))
            self.second = Ring(sems, lambda q, p: buf.at[:, layer(q), p], y, lambda p: device(x, zl, p))
        send, recv = sems.pair()
        self.cross_sems = send, recv
        self.partner = device(x, 1 - zl, y)
        self.other = buf.at[x, 1 - zl, y]

    def cross(self, part, source):
        send, recv = self.cross_sems
        return pltpu.make_async_remote_copy(
            src_ref=source, dst_ref=part, send_sem=send, recv_sem=recv, device_id=self.partner, device_id_type=MESH_ID
        )

    def start(self, source=None):
        source = self.own if source is None else source
        self.sent_cross = self.cross(self.own, source)
        self.sent_cross.start()
        self.first.direct(0, source)

    def crossed(self):
        self.cross(self.other, self.other).wait_recv()
        self.first.direct(1)

    def sent(self):
        self.sent_cross.wait_send()
        self.first.sent()
        self.second.sent()


def split(value):
    high = value.astype(jnp.bfloat16)
    return high, (value - high.astype(jnp.float32)).astype(jnp.bfloat16)


def put_left(ref, value, at=0):
    high, low = split(value)
    for k, part in enumerate((high, low, high)):
        ref[:, at + k * W : at + (k + 1) * W] = part


def put_right(ref, value, col=0, row=0):
    high, low = split(value)
    cols = slice(col, col + value.shape[1])
    for k, part in enumerate((high, high, low)):
        ref[row + k * W : row + (k + 1) * W, cols] = part


def dot(left, right):
    return jnp.dot(left, right, preferred_element_type=jnp.float32)


def panel(buf, s):
    return [(buf[x] if s is None else buf[x, :, :, s]).reshape(B, W) for x in range(4)]


def masked_panel(buf, s, weights):
    return jnp.concatenate([part * weights(x) for x, part in enumerate(panel(buf, s))], axis=0)


def kernel(
    r_in, d_in, l_in, ml_in, j_in, mj_in,
    sol_out, res_out,
    gd, gl, gj0, gj1, gn, gp, rv, ml, mj, mn,
    left_d, left_dt, left_a, left_bt, left_p, left_x, left_j, left_e,
    right_rl, right_lt, right_f, right_b, right_ce, right_x,
    u, xl, f3, w0, xs, rs, c_in, e_in, c_out, e_out,
    send_sem, recv_sem, local_sem,
):
    rhs, node = lax.axis_index("rhs"), lax.axis_index("node")
    x, zl, y = rhs // 8, (rhs // 4) % 2, rhs % 4
    after, before = lax.rem(node + 1, NODES), lax.rem(node + NODES - 1, NODES)
    first, last = node == 0, node == NODES - 1

    def device(px, pz, py):
        return (px * 8 + pz * 4 + py, node)

    sems = Sems(send_sem, recv_sem, local_sem)

    def load(source, target):
        copy = pltpu.make_async_copy(source, target, sems.one())
        copy.start()
        return copy

    ml_load = load(ml_in, ml)
    own_d = load(d_in, gd.at[x, zl, y])
    own_l = load(l_in, gl.at[x, zl, y])
    j_loads = []
    for h, gj in enumerate((gj0, gj1)):
        for s in range(2):
            for c in range(3):
                j_loads.append(load(j_in.at[2 * h + s, :, W * c : W * (c + 1)], gj.at[x, zl, y, 3 * s + c]))
    r_load = load(r_in, rv)
    mj_load = load(mj_in, mj)

    barrier = pltpu.get_barrier_semaphore()
    peers = [device(x, 1 - zl, y)]
    peers += [device(x, zl, lax.rem(y + k, 4)) for k in (1, 3)]
    peers += [device(lax.rem(x + k, 4), zl, y) for k in (1, 3)]
    peers += [(rhs, after), (rhs, before)]
    for peer in peers:
        pl.semaphore_signal(barrier, inc=1, device_id=peer, device_id_type=MESH_ID)
    pl.semaphore_wait(barrier, len(peers))

    gathers = [
        Gather(sems, gd, x, zl, y, device, True),
        Gather(sems, gl, x, zl, y, device, False),
    ]
    later = [
        Gather(sems, gj0, x, zl, y, device, True),
        Gather(sems, gj1, x, zl, y, device, False),
    ]

    def remote(source, target, pair, to):
        return pltpu.make_async_remote_copy(
            src_ref=source,
            dst_ref=target,
            send_sem=pair[0],
            recv_sem=pair[1],
            device_id=(rhs, to),
            device_id_type=MESH_ID,
        )

    for g, source in zip(gathers, (d_in, l_in)):
        g.start(source)
    border = [
        remote(ml_in.at[0], mn, sems.pair(), before),
        remote(gl.at[:, :, :, 0], gn, sems.pair(), before),
        remote(gd.at[:, :, :, 3], gp, sems.pair(), after),
    ]
    border[0].start()
    own_d.wait()
    own_l.wait()
    for g in gathers:
        g.crossed()
    for q in (0, 1):
        for g in gathers:
            g.first.forward(q)
    for q in (0, 1):
        for g in gathers:
            g.first.finish(q)
            g.second.direct(q)
    r_load.wait()
    ml_load.wait()
    for copy in j_loads:
        copy.wait()
    mj_load.wait()
    border[0].wait_recv()
    for q in (0, 1):
        for g in gathers:
            g.second.forward(q)
    for q in (0, 1):
        for g in gathers:
            g.second.finish(q)
    for copy in border[1:]:
        copy.start()

    for g in later:
        g.start()

    for s in range(4):
        d = jnp.concatenate(panel(gd, s), axis=0)
        put_left(left_d.at[s], d)
        put_left(left_dt.at[s], d.T)
        low = masked_panel(gl, s, lambda k: ml[s, k : k + 1, :])
        right = right_rl.at[s]
        put_right(right, rv[W * s : W * (s + 1), :])
        put_right(right, low, W)
        if s == 0:
            put_left(left_e.at[0], -low.T)
        else:
            put_right(right_lt.at[s - 1], low.T)
        both = dot(left_d[s], right[...])
        if s == 0:
            put_right(right_f.at[0], both[:, :W])
            put_right(right_f.at[0], -both[:, W:], W)
        else:
            u[s] = both[:, :W]
            put_left(left_a.at[s], -both[:, W:])
    for s in range(1, 4):
        both = dot(left_a[s], right_f[s - 1])
        fs = u[s] + both[:, :W]
        put_right(right_f.at[s], fs)
        put_right(right_f.at[s], both[:, W:], W)
        if s == 3:
            f3[...] = fs
            put_left(left_p, both[:, W:])

    for g in later:
        g.crossed()

    for s in range(3):
        put_left(left_bt.at[s], -dot(left_dt[s], right_lt[s]))
    for s in range(3, -1, -1):
        both = dot(left_dt[s], right_f[s])
        if s < 3:
            both = both + dot(left_bt[s], right_b[...])
        if s > 0:
            put_right(right_b, both)
        xl[s] = both[:, :W]
        put_left(left_x.at[s], both[:, W:])

    for q in (0, 1):
        for g in later:
            g.first.forward(q)
    for q in (0, 1):
        for g in later:
            g.first.finish(q)
            g.second.direct(q)

    down = [(sems.pair(), slice(HALF * k, HALF * (k + 1))) for k in range(2)]
    up = [(sems.pair(), slice(HALF * k, HALF * (k + 1))) for k in range(2)]

    def send_down(k):
        return remote(c_out.at[k], c_in.at[k], down[k][0], after)

    def send_up(k):
        return remote(e_out.at[k], e_in.at[k], up[k][0], before)

    @pl.when(first)
    def _():
        c_in[...] = jnp.zeros_like(c_in)

    @pl.when(last)
    def _():
        e_in[...] = jnp.zeros_like(e_in)

    for k in range(2):
        cols = down[k][1]

        @pl.when(jnp.logical_not(first))
        def _():
            send_down(k).wait_recv()

        put_right(right_ce, c_in[k], HALF * k)

        @pl.when(jnp.logical_not(last))
        def _():
            c_out[k] = f3[:, cols] + dot(left_p[...], right_ce[: 3 * W, cols])
            send_down(k).start()

    for copy in border[1:]:
        copy.wait_recv()
    nxt = masked_panel(gn, None, lambda k: mn[k : k + 1, :])
    put_right(right_lt.at[3], nxt.T)
    for s in range(3, -1, -1):
        xe = -dot(left_dt[3], right_lt[3]) if s == 3 else dot(left_bt[s], right_b[:, :W])
        if s > 0:
            put_right(right_b, xe)
        put_left(left_x.at[s], xe, 3 * W)

    for k in range(2):
        cols = up[k][1]
        w0[k] = xl[0, :, cols] + dot(left_x[0, :, : 3 * W], right_ce[: 3 * W, cols])

        @pl.when(jnp.logical_not(last))
        def _():
            send_up(k).wait_recv()

        put_right(right_ce, e_in[k], HALF * k, 3 * W)

        @pl.when(jnp.logical_not(first))
        def _():
            e_out[k] = w0[k] + dot(left_x[0, :, 3 * W :], right_ce[3 * W :, cols])
            send_up(k).start()

    for q in (0, 1):
        for g in later:
            g.second.forward(q)

    stores = []
    for s in range(4):
        xa = xl[s] + dot(left_x[s], right_ce[...])
        xs[W * s : W * (s + 1), :] = xa
        put_right(right_x, xa, 0, 3 * W * (s + 1))
    stores.append(pltpu.make_async_copy(xs, sol_out, sems.one()))
    stores[0].start()
    for k in range(2):
        put_right(right_x, e_in[k], HALF * k, 3 * W * 5)
    t = dot(left_e[0], right_x[3 * W : 6 * W, :])
    t = t + jnp.concatenate([c_in[0], c_in[1]], axis=1)

    for q in (0, 1):
        for g in later:
            g.second.finish(q)
    prev = jnp.concatenate(panel(gp, None), axis=0)
    put_left(left_e.at[1], prev.T)
    put_right(right_b, t)
    t = dot(left_e[1], right_b[:, :W])
    put_right(right_x, jnp.where(first, 0.0, t))
    for s in range(4):
        gj = (gj0, gj1)[s // 2]
        for c in range(3):
            block = masked_panel(gj, 3 * (s % 2) + c, lambda k: mj[s, k : k + 1, W * c : W * (c + 1)])
            put_left(left_j, block, 3 * W * c)
        rs[W * s : W * (s + 1), :] = rv[W * s : W * (s + 1), :] - dot(
            left_j[...], right_x[3 * W * s : 3 * W * (s + 3), :]
        )
    stores.append(pltpu.make_async_copy(rs, res_out, sems.one()))
    stores[1].start()

    for g in gathers + later:
        g.sent()
    for copy in border:
        copy.wait_send()

    @pl.when(jnp.logical_not(last))
    def _():
        for k in range(2):
            send_down(k).wait_send()

    @pl.when(jnp.logical_not(first))
    def _():
        for k in range(2):
            send_up(k).wait_send()

    for copy in stores:
        copy.wait()


def on_device(right_side, diag_inv, lower, factor_pattern, jacobian, jacobian_pattern):
    weights_l = jnp.repeat(factor_pattern.astype(jnp.float32), B, axis=2)
    weights_j = jnp.repeat(jacobian_pattern.astype(jnp.float32), B, axis=2)
    f32, bf16 = jnp.float32, jnp.bfloat16
    out = jax.ShapeDtypeStruct(right_side.shape, f32)
    anywhere = pl.BlockSpec(memory_space=pl.ANY)
    vmem = pltpu.VMEM
    return pl.pallas_call(
        kernel,
        out_shape=(out, out),
        in_specs=[anywhere] * 6,
        out_specs=(anywhere, anywhere),
        scratch_shapes=[
            vmem((4, 2, 4, 4, 8, W), f32),
            vmem((4, 2, 4, 4, 8, W), f32),
            vmem((4, 2, 4, 6, 8, W), f32),
            vmem((4, 2, 4, 6, 8, W), f32),
            vmem((4, 2, 4, 8, W), f32),
            vmem((4, 2, 4, 8, W), f32),
            vmem((4 * W, W), f32),
            vmem((4, 4, W), f32),
            vmem((4, 4, 3 * W), f32),
            vmem((4, W), f32),
            vmem((4, W, 3 * W), bf16),
            vmem((4, W, 3 * W), bf16),
            vmem((4, W, 3 * W), bf16),
            vmem((3, W, 3 * W), bf16),
            vmem((W, 3 * W), bf16),
            vmem((4, W, 6 * W), bf16),
            vmem((W, 9 * W), bf16),
            vmem((2, W, 3 * W), bf16),
            vmem((4, 3 * W, 2 * W), bf16),
            vmem((4, 3 * W, W), bf16),
            vmem((4, 3 * W, 2 * W), bf16),
            vmem((3 * W, 2 * W), bf16),
            vmem((6 * W, W), bf16),
            vmem((18 * W, W), bf16),
            vmem((4, W, W), f32),
            vmem((4, W, W), f32),
            vmem((W, W), f32),
            vmem((2, W, HALF), f32),
            vmem((4 * W, W), f32),
            vmem((4 * W, W), f32),
            vmem((2, W, HALF), f32),
            vmem((2, W, HALF), f32),
            vmem((2, W, HALF), f32),
            vmem((2, W, HALF), f32),
            pltpu.SemaphoreType.DMA((64,)),
            pltpu.SemaphoreType.DMA((64,)),
            pltpu.SemaphoreType.DMA((24,)),
        ],
        compiler_params=pltpu.CompilerParams(
            collective_id=0, has_side_effects=True, vmem_limit_bytes=60 * 1024 * 1024
        ),
    )(right_side, diag_inv, lower, weights_l, jacobian, weights_j)


def solution(mesh):
    in_specs = (
        P("node", "rhs"),
        P("node", "rhs", None),
        P("node", "rhs", None),
        P("node", None, None),
        P("node", "rhs", None),
        P("node", None, None),
    )
    out_specs = (P("node", "rhs"), P("node", "rhs"))
    return jax.shard_map(on_device, mesh=mesh, in_specs=in_specs, out_specs=out_specs, check_vma=False)
```

time: 643 us -> 103 us (0.16)
  waiting for transfers between devices: 384 us -> 0 us
  matrix products: 133 us -> 0 us
  Pallas kernels: 0 us -> 96.7 us
  starting transfers between devices: 82.5 us -> 0 us
  between operations: 13.9 us -> 0.67 us
  local copies, waits for them, and re-layouts: 17.9 us -> 4.92 us
    all_gather x3 -> x0, waiting for transfers between devices: 284 us -> none  [the longest x1 153 us: on_device(): lax.all_gather(diag_inv, 'rhs', axis=1, tiled=True)]
    dot_general x130 -> x0, matrix products: 133 us -> none  [the longest x32 52.3 us: advance(): lax.dot_general(inv_block, forward_block - entering, TRANSPOSED, precisio...]
    ppermute x16 -> x0, waiting for transfers between devices: 98.7 us -> none  [the longest x14 88.2 us: shifted(): lax.ppermute(value, axis, [(source, source + steps) for source in range(i...]
    pallas_call x0 -> x1, Pallas kernels: none -> 96.7 us  [on_device(): pl.pallas_call(kernel, out_shape=(out, out), in_specs=[anywhere] * 6, out...]
    ppermute x16 -> x0, starting transfers between devices: 82.4 us -> none  [the longest x14 74.5 us: shifted(): lax.ppermute(value, axis, [(source, source + steps) for source in range(i...]
    while x14 -> x0, local copies, waits for them, and re-layouts: 6.78 us -> none
  transfers between devices with their start and end apart: 19 -> 0, of which waited for: 18 -> 0; matrix products, arithmetic and copies ran while one was open for 22% -> 0% of each run, Pallas kernels for 0% -> 0%
where the time goes in v1:
time: 103 us
  Pallas kernels  96.7 us (94%)
  local copies, waits for them, and re-layouts  4.92 us (5%)
    pallas_call x1, Pallas kernels, on_device(): pl.pallas_call(kernel, out_shape=(out, out), in_specs=[anywhere] * 6, out...  96.7 us
    unnamed x6, local copies, waits for them, and re-layouts  3.33 us

profile of v1, /device:TPU:1, one launch (start us, length us, event | category | flops | bytes accessed | tf_op | source)
XLA Modules:
  0.0 103.0 jit_solution(1917149912043987127)
XLA Ops:
  0.6 0.0 copy-start.1
  0.6 0.7 convert_element_type.6
  1.3 0.0 copy-done.1
  1.4 0.1 broadcast_in_dim.6
  1.4 0.7 reshape.10.ml_in
  2.1 0.1 broadcast_in_dim.7
  2.2 0.7 reshape.11.mj_in
  3.0 96.7 %shard_map.77 = (f32[1024,256]{1,0:T(8,128)}, f32[1024,256]{1,0:T(8,128)}) custom-call(f32[1024,256]{1,0:T(8,128)} %r_in.1, f32[4,8,256]{2,1,0:T(8,128)} %d_in.1, f32[4,8,256]{2,1,0:T(8,128)} %l_in.1, f32[4,4,256]{2,1,0:T(4,128)} %reshape.10.ml_in, f32[4,8,768]{2,1,0:T(8,128)} %j_in.1, f32[4,4,768]{2,1,0:T(4,128)} %reshape.11.mj_in), custom_call_target="tpu_custom_call" | custom-call | tf_op jit(solution)/shard_map/pallas_call | solution.py:421
  99.7 0.0 copy-start
  99.7 2.4 %copy.10 = f32[1024,256]{1,0:T(8,128)} copy(f32[1024,256]{1,0:T(8,128)} %get-tuple-element.4) | data formatting | bytes 2097152
  102.0 0.0 copy-done
  102.0 1.0 copy.11
  (1 shorter events, 0.0 us)
Async XLA Ops:
  0.6 0.7 copy-start.1
  99.7 2.4 %copy-start = (f32[1024,256]{1,0:T(8,128)S(1)}, f32[1024,256]{1,0:T(8,128)}, u32[]{:S(2)}) copy-start(f32[1024,256]{1,0:T(8,128)} %get-tuple-element.5) | copy-start | bytes 3145732

commit v2 on v1

--- a/solution.py
+++ b/solution.py
@@ -33,7 +33,7 @@
         self.where, self.pos = where, pos
         self.up, self.down = device_at(lax.rem(pos + 1, 4)), device_at(lax.rem(pos + 3, 4))
         self.sems = {key: sems.pair() for key in ("u0", "d0", "u1", "d1", "fu", "fd")}
-        self.started = []
+        self.started = {}
 
     def at(self, q, step):
         return self.where(q, lax.rem(self.pos + step, 4))
@@ -50,10 +50,9 @@
             device_id_type=MESH_ID,
         )
 
-    def go(self, *args):
-        copy = self.copy(*args)
-        copy.start()
-        self.started.append(copy)
+    def go(self, key, *args):
+        self.started[key] = args
+        self.copy(key, *args).start()
 
     def direct(self, q, source=None):
         first, second = ("u", "d") if q == 0 else ("d", "u")
@@ -77,8 +76,8 @@
             self.copy("fd", 1, 2, self.down).wait_recv()
 
     def sent(self):
-        for copy in self.started:
-            copy.wait_send()
+        for key, args in self.started.items():
+            self.copy(key, *args).wait_send()
 
 
 class Gather:
@@ -151,13 +150,22 @@
     return jnp.concatenate([part * weights(x) for x, part in enumerate(panel(buf, s))], axis=0)
 
 
+def rows_of(pattern):
+    block = lax.broadcasted_iota(jnp.int32, (4, W), 1) // B
+    values = pattern.astype(jnp.float32)
+    out = jnp.zeros((4, W), jnp.float32)
+    for k in range(4):
+        out = jnp.where(block == k, values[:, k : k + 1], out)
+    return out
+
+
 def kernel(
-    r_in, d_in, l_in, ml_in, j_in, mj_in,
-    sol_out, res_out,
-    gd, gl, gj0, gj1, gn, gp, rv, ml, mj, mn,
+    r_in, d_in, l_in, pl_in, j_in, pj_in,
+    xs, rs,
+    gd, gl, gj0, gj1, gn, gp, rv, pat_l, pat_j, ml, mj, mn,
     left_d, left_dt, left_a, left_bt, left_p, left_x, left_j, left_e,
     right_rl, right_lt, right_f, right_b, right_ce, right_x,
-    u, xl, f3, w0, xs, rs, c_in, e_in, c_out, e_out,
+    u, xl, f3, w0, c_in, e_in, c_out, e_out,
     send_sem, recv_sem, local_sem,
 ):
     rhs, node = lax.axis_index("rhs"), lax.axis_index("node")
@@ -174,17 +182,6 @@
         copy = pltpu.make_async_copy(source, target, sems.one())
         copy.start()
         return copy
-
-    ml_load = load(ml_in, ml)
-    own_d = load(d_in, gd.at[x, zl, y])
-    own_l = load(l_in, gl.at[x, zl, y])
-    j_loads = []
-    for h, gj in enumerate((gj0, gj1)):
-        for s in range(2):
-            for c in range(3):
-                j_loads.append(load(j_in.at[2 * h + s, :, W * c : W * (c + 1)], gj.at[x, zl, y, 3 * s + c]))
-    r_load = load(r_in, rv)
-    mj_load = load(mj_in, mj)
 
     barrier = pltpu.get_barrier_semaphore()
     peers = [device(x, 1 - zl, y)]
@@ -217,11 +214,19 @@
     for g, source in zip(gathers, (d_in, l_in)):
         g.start(source)
     border = [
-        remote(ml_in.at[0], mn, sems.pair(), before),
+        remote(ml.at[0], mn, sems.pair(), before),
         remote(gl.at[:, :, :, 0], gn, sems.pair(), before),
         remote(gd.at[:, :, :, 3], gp, sems.pair(), after),
     ]
-    border[0].start()
+    own_d = load(d_in, gd.at[x, zl, y])
+    own_l = load(l_in, gl.at[x, zl, y])
+    pat_loads = [load(pl_in, pat_l), load(pj_in, pat_j)]
+    j_loads = []
+    for h, gj in enumerate((gj0, gj1)):
+        for s in range(2):
+            for c in range(3):
+                j_loads.append(load(j_in.at[2 * h + s, :, W * c : W * (c + 1)], gj.at[x, zl, y, 3 * s + c]))
+    r_load = load(r_in, rv)
     own_d.wait()
     own_l.wait()
     for g in gathers:
@@ -234,18 +239,19 @@
             g.first.finish(q)
             g.second.direct(q)
     r_load.wait()
-    ml_load.wait()
-    for copy in j_loads:
+    for copy in pat_loads + j_loads:
         copy.wait()
-    mj_load.wait()
-    border[0].wait_recv()
+    for s in range(4):
+        ml[s] = rows_of(pat_l[s])
+        for c in range(3):
+            mj[s, :, W * c : W * (c + 1)] = rows_of(pat_j[s, :, 4 * c : 4 * (c + 1)])
     for q in (0, 1):
         for g in gathers:
             g.second.forward(q)
     for q in (0, 1):
         for g in gathers:
             g.second.finish(q)
-    for copy in border[1:]:
+    for copy in border[:2]:
         copy.start()
 
     for g in later:
@@ -279,8 +285,39 @@
             f3[...] = fs
             put_left(left_p, both[:, W:])
 
-    for g in later:
-        g.crossed()
+    chunks = [slice(HALF * k, HALF * (k + 1)) for k in range(2)]
+    down = [sems.pair() for k in range(2)]
+    up = [sems.pair() for k in range(2)]
+
+    def send_down(k):
+        return remote(c_out.at[k], c_in.at[k], down[k], after)
+
+    def send_up(k):
+        return remote(e_out.at[k], e_in.at[k], up[k], before)
+
+    @pl.when(first)
+    def _():
+        c_in[...] = jnp.zeros_like(c_in)
+
+    @pl.when(last)
+    def _():
+        e_in[...] = jnp.zeros_like(e_in)
+
+    def relay_down():
+        for k, cols in enumerate(chunks):
+
+            @pl.when(jnp.logical_not(first))
+            def _():
+                send_down(k).wait_recv()
+
+            put_right(right_ce, c_in[k], HALF * k)
+
+            @pl.when(jnp.logical_not(last))
+            def _():
+                c_out[k] = f3[:, cols] + dot(left_p[...], right_ce[: 3 * W, cols])
+                send_down(k).start()
+
+    pl.when(node < 2)(relay_down)
 
     for s in range(3):
         put_left(left_bt.at[s], -dot(left_dt[s], right_lt[s]))
@@ -293,6 +330,10 @@
         xl[s] = both[:, :W]
         put_left(left_x.at[s], both[:, W:])
 
+    pl.when((node == 2) | (node == 3))(relay_down)
+
+    for g in later:
+        g.crossed()
     for q in (0, 1):
         for g in later:
             g.first.forward(q)
@@ -301,38 +342,10 @@
             g.first.finish(q)
             g.second.direct(q)
 
-    down = [(sems.pair(), slice(HALF * k, HALF * (k + 1))) for k in range(2)]
-    up = [(sems.pair(), slice(HALF * k, HALF * (k + 1))) for k in range(2)]
-
-    def send_down(k):
-        return remote(c_out.at[k], c_in.at[k], down[k][0], after)
-
-    def send_up(k):
-        return remote(e_out.at[k], e_in.at[k], up[k][0], before)
-
-    @pl.when(first)
-    def _():
-        c_in[...] = jnp.zeros_like(c_in)
-
-    @pl.when(last)
-    def _():
-        e_in[...] = jnp.zeros_like(e_in)
-
-    for k in range(2):
-        cols = down[k][1]
-
-        @pl.when(jnp.logical_not(first))
-        def _():
-            send_down(k).wait_recv()
-
-        put_right(right_ce, c_in[k], HALF * k)
-
-        @pl.when(jnp.logical_not(last))
-        def _():
-            c_out[k] = f3[:, cols] + dot(left_p[...], right_ce[: 3 * W, cols])
-            send_down(k).start()
-
-    for copy in border[1:]:
+    pl.when(node > 3)(relay_down)
+
+    border[2].start()
+    for copy in border[:2]:
         copy.wait_recv()
     nxt = masked_panel(gn, None, lambda k: mn[k : k + 1, :])
     put_right(right_lt.at[3], nxt.T)
@@ -342,8 +355,14 @@
             put_right(right_b, xe)
         put_left(left_x.at[s], xe, 3 * W)
 
-    for k in range(2):
-        cols = up[k][1]
+    def forward_later():
+        for q in (0, 1):
+            for g in later:
+                g.second.forward(q)
+
+    pl.when(jnp.logical_not(last))(forward_later)
+
+    for k, cols in enumerate(chunks):
         w0[k] = xl[0, :, cols] + dot(left_x[0, :, : 3 * W], right_ce[: 3 * W, cols])
 
         @pl.when(jnp.logical_not(last))
@@ -357,17 +376,12 @@
             e_out[k] = w0[k] + dot(left_x[0, :, 3 * W :], right_ce[3 * W :, cols])
             send_up(k).start()
 
-    for q in (0, 1):
-        for g in later:
-            g.second.forward(q)
-
-    stores = []
+    pl.when(last)(forward_later)
+
     for s in range(4):
         xa = xl[s] + dot(left_x[s], right_ce[...])
         xs[W * s : W * (s + 1), :] = xa
         put_right(right_x, xa, 0, 3 * W * (s + 1))
-    stores.append(pltpu.make_async_copy(xs, sol_out, sems.one()))
-    stores[0].start()
     for k in range(2):
         put_right(right_x, e_in[k], HALF * k, 3 * W * 5)
     t = dot(left_e[0], right_x[3 * W : 6 * W, :])
@@ -376,6 +390,7 @@
     for q in (0, 1):
         for g in later:
             g.second.finish(q)
+    border[2].wait_recv()
     prev = jnp.concatenate(panel(gp, None), axis=0)
     put_left(left_e.at[1], prev.T)
     put_right(right_b, t)
@@ -389,8 +404,6 @@
         rs[W * s : W * (s + 1), :] = rv[W * s : W * (s + 1), :] - dot(
             left_j[...], right_x[3 * W * s : 3 * W * (s + 3), :]
         )
-    stores.append(pltpu.make_async_copy(rs, res_out, sems.one()))
-    stores[1].start()
 
     for g in gathers + later:
         g.sent()
@@ -407,22 +420,17 @@
         for k in range(2):
             send_up(k).wait_send()
 
-    for copy in stores:
-        copy.wait()
-
-
-def on_device(right_side, diag_inv, lower, factor_pattern, jacobian, jacobian_pattern):
-    weights_l = jnp.repeat(factor_pattern.astype(jnp.float32), B, axis=2)
-    weights_j = jnp.repeat(jacobian_pattern.astype(jnp.float32), B, axis=2)
+
+def on_device(*args):
     f32, bf16 = jnp.float32, jnp.bfloat16
-    out = jax.ShapeDtypeStruct(right_side.shape, f32)
-    anywhere = pl.BlockSpec(memory_space=pl.ANY)
+    out = jax.ShapeDtypeStruct(args[0].shape, f32)
+    hbm = pl.BlockSpec(memory_space=pltpu.HBM)
     vmem = pltpu.VMEM
     return pl.pallas_call(
         kernel,
         out_shape=(out, out),
-        in_specs=[anywhere] * 6,
-        out_specs=(anywhere, anywhere),
+        in_specs=[hbm] * 6,
+        out_specs=(pl.BlockSpec(memory_space=vmem),) * 2,
         scratch_shapes=[
             vmem((4, 2, 4, 4, 8, W), f32),
             vmem((4, 2, 4, 4, 8, W), f32),
@@ -431,6 +439,8 @@
             vmem((4, 2, 4, 8, W), f32),
             vmem((4, 2, 4, 8, W), f32),
             vmem((4 * W, W), f32),
+            vmem((4, 4, 4), jnp.int32),
+            vmem((4, 4, 12), jnp.int32),
             vmem((4, 4, W), f32),
             vmem((4, 4, 3 * W), f32),
             vmem((4, W), f32),
@@ -452,8 +462,6 @@
             vmem((4, W, W), f32),
             vmem((W, W), f32),
             vmem((2, W, HALF), f32),
-            vmem((4 * W, W), f32),
-            vmem((4 * W, W), f32),
             vmem((2, W, HALF), f32),
             vmem((2, W, HALF), f32),
             vmem((2, W, HALF), f32),
@@ -463,9 +471,9 @@
             pltpu.SemaphoreType.DMA((24,)),
         ],
         compiler_params=pltpu.CompilerParams(
-            collective_id=0, has_side_effects=True, vmem_limit_bytes=60 * 1024 * 1024
+            collective_id=0, has_side_effects=True, vmem_limit_bytes=48 * 1024 * 1024
         ),
-    )(right_side, diag_inv, lower, weights_l, jacobian, weights_j)
+    )(*[pltpu.with_memory_space_constraint(a, pltpu.HBM) for a in args])
 
 
 def solution(mesh):

time: 103 us -> 84.6 us (0.82)
  the two profiles are of different devices: /device:TPU:1 before, /device:TPU:32 now
where the time goes in v2:
time: 84.6 us; the launch traced here: 84.5 us
  Pallas kernels  81.9 us (97%)
  local copies, waits for them, and re-layouts  1.94 us (2%)
    pallas_call x1, Pallas kernels, on_device(): pl.pallas_call(kernel, out_shape=(out, out), in_specs=[hbm] * 6, out_spec...  81.9 us
    unnamed x2, local copies, waits for them, and re-layouts  1.94 us

profile of v2, /device:TPU:32, one launch (start us, length us, event | category | flops | bytes accessed | tf_op | source)
XLA Modules:
  0.0 84.5 jit_solution(11679260509824768177)
XLA Ops:
  0.6 81.9 %shard_map.77 = (f32[1024,256]{1,0:T(8,128)S(1)}, f32[1024,256]{1,0:T(8,128)S(1)}) custom-call(f32[1024,256]{1,0:T(8,128)} %r_in.1, f32[4,8,256]{2,1,0:T(8,128)} %d_in.1, f32[4,8,256]{2,1,0:T(8,128)} %l_in.1, s32[4,4,4]{2,1,0:T(4,128)} %pl_in.1, f32[4,8,768]{2,1,0:T(8,128)} %j_in.1, s32[4,4,12]{2,1,0:T(4,128)} %pj_in.1), custom_call_target="tpu_custom_call" | custom-call | tf_op jit(solution)/shard_map/pallas_call | solution.py:429
  82.6 1.0 %copy.10 = f32[1024,256]{1,0:T(8,128)} copy(f32[1024,256]{1,0:T(8,128)S(1)} %get-tuple-element.4) | data formatting | bytes 2097152
  83.5 1.0 %copy.11 = f32[1024,256]{1,0:T(8,128)} copy(f32[1024,256]{1,0:T(8,128)S(1)} %get-tuple-element.5) | data formatting | bytes 2097152

commit v3 on v2

--- a/solution.py
+++ b/solution.py
@@ -9,7 +9,8 @@
 B = 64
 W = 256
 NODES = 8
-HALF = 128
+CHUNKS = 4
+PART = W // CHUNKS
 
 
 class Sems:
@@ -163,15 +164,19 @@
     r_in, d_in, l_in, pl_in, j_in, pj_in,
     xs, rs,
     gd, gl, gj0, gj1, gn, gp, rv, pat_l, pat_j, ml, mj, mn,
-    left_d, left_dt, left_a, left_bt, left_p, left_x, left_j, left_e,
-    right_rl, right_lt, right_f, right_b, right_ce, right_x,
-    u, xl, f3, w0, c_in, e_in, c_out, e_out,
+    left_d, left_dt, left_a, left_bt, left_x, left_j, left_e, left_r, left_m, left_g, left_n,
+    right_rl, right_lt, right_f, right_b, right_x, right_p, right_q, right_g, right_u, right_c, right_e,
+    u, xl, gt, pt, ga, pa, gg, ct, cn, w0, x0, wb, xb, ht, en, c_in, e_in, c_out, e_out,
     send_sem, recv_sem, local_sem,
 ):
     rhs, node = lax.axis_index("rhs"), lax.axis_index("node")
     x, zl, y = rhs // 8, (rhs // 4) % 2, rhs % 4
     after, before = lax.rem(node + 1, NODES), lax.rem(node + NODES - 1, NODES)
-    first, last = node == 0, node == NODES - 1
+    first = node == 0
+    chip, odd = node // 2, node % 2 == 1
+    even = jnp.logical_not(odd)
+    partner = node + 1 - 2 * (node % 2)
+    two_after, two_before = lax.rem(node + 2, NODES), lax.rem(node + NODES - 2, NODES)
 
     def device(px, pz, py):
         return (px * 8 + pz * 4 + py, node)
@@ -187,7 +192,7 @@
     peers = [device(x, 1 - zl, y)]
     peers += [device(x, zl, lax.rem(y + k, 4)) for k in (1, 3)]
     peers += [device(lax.rem(x + k, 4), zl, y) for k in (1, 3)]
-    peers += [(rhs, after), (rhs, before)]
+    peers += [(rhs, to) for to in (after, before, two_after, two_before)]
     for peer in peers:
         pl.semaphore_signal(barrier, inc=1, device_id=peer, device_id_type=MESH_ID)
     pl.semaphore_wait(barrier, len(peers))
@@ -282,42 +287,75 @@
         put_right(right_f.at[s], fs)
         put_right(right_f.at[s], both[:, W:], W)
         if s == 3:
-            f3[...] = fs
-            put_left(left_p, both[:, W:])
-
-    chunks = [slice(HALF * k, HALF * (k + 1)) for k in range(2)]
-    down = [sems.pair() for k in range(2)]
-    up = [sems.pair() for k in range(2)]
+            gt[...] = fs.T
+            pt[...] = both[:, W:].T
+
+    chunks = [slice(PART * k, PART * (k + 1)) for k in range(CHUNKS)]
+    down, fan_down, up, fan_up = [[sems.pair() for k in range(CHUNKS)] for _ in range(4)]
+    hand = [
+        remote(gt, ga, sems.pair(), partner),
+        remote(pt, pa, sems.pair(), partner),
+        remote(w0, wb, sems.pair(), partner),
+        remote(x0, xb, sems.pair(), partner),
+    ]
 
     def send_down(k):
-        return remote(c_out.at[k], c_in.at[k], down[k], after)
+        return remote(c_out.at[k], c_in.at[k], down[k], two_after)
+
+    def share_down(k):
+        return remote(c_in.at[k], c_in.at[k], fan_down[k], partner)
 
     def send_up(k):
-        return remote(e_out.at[k], e_in.at[k], up[k], before)
-
-    @pl.when(first)
+        return remote(e_out.at[k], e_in.at[k], up[k], two_before)
+
+    def share_up(k):
+        return remote(e_in.at[k], e_in.at[k], fan_up[k], partner)
+
+    @pl.when(even)
+    def _():
+        hand[0].start()
+        hand[1].start()
+
+    @pl.when(chip == 0)
     def _():
         c_in[...] = jnp.zeros_like(c_in)
-
-    @pl.when(last)
+        left_m[...] = jnp.zeros_like(left_m)
+
+    @pl.when(chip == 3)
     def _():
         e_in[...] = jnp.zeros_like(e_in)
 
+    @pl.when(odd)
+    def _():
+        put_right(right_p, pt[...])
+        hand[0].wait_recv()
+        put_left(left_g, ga[...])
+        gg[...] = gt[...] + dot(left_g[...], right_p[...])
+
+    @pl.when(odd & (chip == 0))
+    def _():
+        for k, rows in enumerate(chunks):
+            c_out[k] = gg[rows, :]
+            send_down(k).start()
+
+    @pl.when(odd)
+    def _():
+        hand[1].wait_recv()
+        put_left(left_g, pa[...])
+        put_right(right_g, pa[...])
+        put_right(right_q, dot(left_g[...], right_p[...]))
+
     def relay_down():
-        for k, cols in enumerate(chunks):
-
-            @pl.when(jnp.logical_not(first))
+        for k, rows in enumerate(chunks):
+            send_down(k).wait_recv()
+            put_left(left_m.at[rows], c_in[k])
+
+            @pl.when(chip < 3)
             def _():
-                send_down(k).wait_recv()
-
-            put_right(right_ce, c_in[k], HALF * k)
-
-            @pl.when(jnp.logical_not(last))
-            def _():
-                c_out[k] = f3[:, cols] + dot(left_p[...], right_ce[: 3 * W, cols])
+                c_out[k] = gg[rows, :] + dot(left_m[rows, :], right_q[...])
                 send_down(k).start()
 
-    pl.when(node < 2)(relay_down)
+            share_down(k).start()
 
     for s in range(3):
         put_left(left_bt.at[s], -dot(left_dt[s], right_lt[s]))
@@ -330,10 +368,10 @@
         xl[s] = both[:, :W]
         put_left(left_x.at[s], both[:, W:])
 
-    pl.when((node == 2) | (node == 3))(relay_down)
-
     for g in later:
         g.crossed()
+    pl.when(odd & (chip == 1))(relay_down)
+
     for q in (0, 1):
         for g in later:
             g.first.forward(q)
@@ -342,83 +380,166 @@
             g.first.finish(q)
             g.second.direct(q)
 
-    pl.when(node > 3)(relay_down)
-
-    border[2].start()
     for copy in border[:2]:
         copy.wait_recv()
     nxt = masked_panel(gn, None, lambda k: mn[k : k + 1, :])
     put_right(right_lt.at[3], nxt.T)
     for s in range(3, -1, -1):
-        xe = -dot(left_dt[3], right_lt[3]) if s == 3 else dot(left_bt[s], right_b[:, :W])
-        if s > 0:
-            put_right(right_b, xe)
+        if s == 3:
+            xe = -dot(left_dt[3], right_lt[3])
+        else:
+            xe = dot(left_bt[s], right_x[3 * W * (s + 2) : 3 * W * (s + 3), W:])
+        put_right(right_x, xe, W, 3 * W * (s + 1))
         put_left(left_x.at[s], xe, 3 * W)
+        if s == 0:
+            x0[...] = xe
+
+    @pl.when(odd)
+    def _():
+        hand[3].start()
+
+    @pl.when(even)
+    def _():
+        hand[3].wait_recv()
+        put_left(left_n, xb[...])
+        put_right(right_b, xb[...])
+        both = dot(left_x[0, :, 3 * W :], right_b[:, :W])
+        put_right(right_u, both.T)
+
+    pl.when(odd & (chip > 1))(relay_down)
+
+    @pl.when(odd)
+    def _():
+        ct[...] = ga[...] + dot(left_m[...], right_g[...])
+
+    @pl.when(even & (chip > 0))
+    def _():
+        for k in range(CHUNKS):
+            share_down(k).wait_recv()
+
+    @pl.when(even)
+    def _():
+        ct[...] = c_in[...].reshape(W, W)
+
+    cn[...] = ct[...].T
+    put_right(right_c, cn[...])
+    xl[0] = xl[0] + dot(left_x[0, :, : 3 * W], right_c[...])
+
+    @pl.when(odd)
+    def _():
+        w0[...] = xl[0]
+        hand[2].start()
+
+    border[2].start()
+
+    @pl.when(even)
+    def _():
+        hand[2].wait_recv()
+        put_right(right_b, wb[...])
+        both = dot(left_x[0, :, 3 * W :], right_b[:, :W])
+        ht[...] = (xl[0] + both).T
 
     def forward_later():
         for q in (0, 1):
             for g in later:
                 g.second.forward(q)
 
-    pl.when(jnp.logical_not(last))(forward_later)
-
-    for k, cols in enumerate(chunks):
-        w0[k] = xl[0, :, cols] + dot(left_x[0, :, : 3 * W], right_ce[: 3 * W, cols])
-
-        @pl.when(jnp.logical_not(last))
-        def _():
-            send_up(k).wait_recv()
-
-        put_right(right_ce, e_in[k], HALF * k, 3 * W)
-
-        @pl.when(jnp.logical_not(first))
-        def _():
-            e_out[k] = w0[k] + dot(left_x[0, :, 3 * W :], right_ce[3 * W :, cols])
-            send_up(k).start()
-
-    pl.when(last)(forward_later)
-
+    def prepare():
+        for s in range(4):
+            if s > 0:
+                xl[s] = xl[s] + dot(left_x[s, :, : 3 * W], right_c[...])
+            put_right(right_x, xl[s], 0, 3 * W * (s + 1))
+        diagonal = lax.broadcasted_iota(jnp.int32, (W, W), 0) == lax.broadcasted_iota(jnp.int32, (W, W), 1)
+        put_right(right_x, jnp.zeros((W, W), jnp.float32), 0, 15 * W)
+        put_right(right_x, diagonal.astype(jnp.float32), W, 15 * W)
+        border[2].wait_recv()
+        prev = jnp.concatenate(panel(gp, None), axis=0)
+        put_left(left_e.at[1], prev.T)
+        both = dot(left_e[0], right_x[3 * W : 6 * W, :])
+        put_right(right_b, both[:, :W] + cn[...])
+        put_right(right_b, both[:, W:], W)
+        both = dot(left_e[1], right_b[...])
+        put_right(right_x, jnp.where(first, 0.0, both))
+        for q in (0, 1):
+            for g in later:
+                g.second.finish(q)
+        for s in range(4):
+            gj = (gj0, gj1)[s // 2]
+            for c in range(3):
+                block = masked_panel(gj, 3 * (s % 2) + c, lambda k: mj[s, k : k + 1, W * c : W * (c + 1)])
+                put_left(left_j, block, 3 * W * c)
+            both = dot(left_j[...], right_x[3 * W * s : 3 * W * (s + 3), :])
+            rs[W * s : W * (s + 1), :] = rv[W * s : W * (s + 1), :] - both[:, :W]
+            put_left(left_r.at[s], -both[:, W:])
+
+    pl.when(chip < 3)(forward_later)
+    pl.when(chip < 2)(prepare)
+
+    @pl.when(even)
+    def _():
+        for k, rows in enumerate(chunks):
+
+            @pl.when(chip < 3)
+            def _():
+                send_up(k).wait_recv()
+
+            @pl.when(chip > 0)
+            def _():
+                put_left(left_m.at[rows], e_in[k])
+                e_out[k] = ht[rows, :] + dot(left_m[rows, :], right_u[...])
+                send_up(k).start()
+
+            @pl.when(chip < 3)
+            def _():
+                share_up(k).start()
+
+    pl.when(chip == 3)(forward_later)
+    pl.when(chip > 1)(prepare)
+
+    @pl.when(odd & (chip < 3))
+    def _():
+        for k in range(CHUNKS):
+            share_up(k).wait_recv()
+
+    en[...] = e_in[...].reshape(W, W).T
+
+    @pl.when(even)
+    def _():
+        put_right(right_b, en[...])
+        en[...] = wb[...] + dot(left_n[...], right_b[:, :W])
+
+    put_right(right_e, en[...])
     for s in range(4):
-        xa = xl[s] + dot(left_x[s], right_ce[...])
-        xs[W * s : W * (s + 1), :] = xa
-        put_right(right_x, xa, 0, 3 * W * (s + 1))
-    for k in range(2):
-        put_right(right_x, e_in[k], HALF * k, 3 * W * 5)
-    t = dot(left_e[0], right_x[3 * W : 6 * W, :])
-    t = t + jnp.concatenate([c_in[0], c_in[1]], axis=1)
-
-    for q in (0, 1):
-        for g in later:
-            g.second.finish(q)
-    border[2].wait_recv()
-    prev = jnp.concatenate(panel(gp, None), axis=0)
-    put_left(left_e.at[1], prev.T)
-    put_right(right_b, t)
-    t = dot(left_e[1], right_b[:, :W])
-    put_right(right_x, jnp.where(first, 0.0, t))
-    for s in range(4):
-        gj = (gj0, gj1)[s // 2]
-        for c in range(3):
-            block = masked_panel(gj, 3 * (s % 2) + c, lambda k: mj[s, k : k + 1, W * c : W * (c + 1)])
-            put_left(left_j, block, 3 * W * c)
-        rs[W * s : W * (s + 1), :] = rv[W * s : W * (s + 1), :] - dot(
-            left_j[...], right_x[3 * W * s : 3 * W * (s + 3), :]
-        )
+        rows = slice(W * s, W * (s + 1))
+        xs[rows, :] = xl[s] + dot(left_x[s, :, 3 * W :], right_e[...])
+        rs[rows, :] = rs[rows, :] + dot(left_r[s], right_e[...])
 
     for g in gathers + later:
         g.sent()
     for copy in border:
         copy.wait_send()
 
-    @pl.when(jnp.logical_not(last))
-    def _():
-        for k in range(2):
-            send_down(k).wait_send()
-
-    @pl.when(jnp.logical_not(first))
-    def _():
-        for k in range(2):
-            send_up(k).wait_send()
+    def sent(cond, *copies):
+        @pl.when(cond)
+        def _():
+            for copy in copies:
+                for k in range(CHUNKS):
+                    copy(k).wait_send()
+
+    sent(odd & (chip < 3), send_down)
+    sent(odd & (chip > 0), share_down)
+    sent(even & (chip > 0), send_up)
+    sent(even & (chip < 3), share_up)
+
+    @pl.when(even)
+    def _():
+        hand[0].wait_send()
+        hand[1].wait_send()
+
+    @pl.when(odd)
+    def _():
+        hand[2].wait_send()
+        hand[3].wait_send()
 
 
 def on_device(*args):
@@ -448,26 +569,45 @@
             vmem((4, W, 3 * W), bf16),
             vmem((4, W, 3 * W), bf16),
             vmem((3, W, 3 * W), bf16),
-            vmem((W, 3 * W), bf16),
             vmem((4, W, 6 * W), bf16),
             vmem((W, 9 * W), bf16),
             vmem((2, W, 3 * W), bf16),
+            vmem((4, W, 3 * W), bf16),
+            vmem((W, 3 * W), bf16),
+            vmem((W, 3 * W), bf16),
+            vmem((W, 3 * W), bf16),
             vmem((4, 3 * W, 2 * W), bf16),
             vmem((4, 3 * W, W), bf16),
             vmem((4, 3 * W, 2 * W), bf16),
             vmem((3 * W, 2 * W), bf16),
-            vmem((6 * W, W), bf16),
-            vmem((18 * W, W), bf16),
+            vmem((18 * W, 2 * W), bf16),
+            vmem((3 * W, W), bf16),
+            vmem((3 * W, W), bf16),
+            vmem((3 * W, W), bf16),
+            vmem((3 * W, W), bf16),
+            vmem((3 * W, W), bf16),
+            vmem((3 * W, W), bf16),
             vmem((4, W, W), f32),
             vmem((4, W, W), f32),
             vmem((W, W), f32),
-            vmem((2, W, HALF), f32),
-            vmem((2, W, HALF), f32),
-            vmem((2, W, HALF), f32),
-            vmem((2, W, HALF), f32),
-            vmem((2, W, HALF), f32),
-            pltpu.SemaphoreType.DMA((64,)),
-            pltpu.SemaphoreType.DMA((64,)),
+            vmem((W, W), f32),
+            vmem((W, W), f32),
+            vmem((W, W), f32),
+            vmem((W, W), f32),
+            vmem((W, W), f32),
+            vmem((W, W), f32),
+            vmem((W, W), f32),
+            vmem((W, W), f32),
+            vmem((W, W), f32),
+            vmem((W, W), f32),
+            vmem((W, W), f32),
+            vmem((W, W), f32),
+            vmem((CHUNKS, PART, W), f32),
+            vmem((CHUNKS, PART, W), f32),
+            vmem((CHUNKS, PART, W), f32),
+            vmem((CHUNKS, PART, W), f32),
+            pltpu.SemaphoreType.DMA((76,)),
+            pltpu.SemaphoreType.DMA((76,)),
             pltpu.SemaphoreType.DMA((24,)),
         ],
         compiler_params=pltpu.CompilerParams(

time: 84.6 us -> 74.5 us (0.88)
  the two profiles are of different devices: /device:TPU:32 before, /device:TPU:33 now
where the time goes in v3:
time: 74.5 us; the launch traced here: 74.4 us
  Pallas kernels  71.8 us (96%)
  local copies, waits for them, and re-layouts  1.94 us (3%)
    pallas_call x1, Pallas kernels, on_device(): pl.pallas_call(kernel, out_shape=(out, out), in_specs=[hbm] * 6, out_spec...  71.8 us
    unnamed x2, local copies, waits for them, and re-layouts  1.94 us

profile of v3, /device:TPU:33, one launch (start us, length us, event | category | flops | bytes accessed | tf_op | source)
XLA Modules:
  0.0 74.4 jit_solution(6840407049417470094)
XLA Ops:
  0.6 71.8 %shard_map.77 = (f32[1024,256]{1,0:T(8,128)S(1)}, f32[1024,256]{1,0:T(8,128)S(1)}) custom-call(f32[1024,256]{1,0:T(8,128)} %r_in.1, f32[4,8,256]{2,1,0:T(8,128)} %d_in.1, f32[4,8,256]{2,1,0:T(8,128)} %l_in.1, s32[4,4,4]{2,1,0:T(4,128)} %pl_in.1, f32[4,8,768]{2,1,0:T(8,128)} %j_in.1, s32[4,4,12]{2,1,0:T(4,128)} %pj_in.1), custom_call_target="tpu_custom_call" | custom-call | tf_op jit(solution)/shard_map/pallas_call | solution.py:550
  72.4 1.0 %copy.10 = f32[1024,256]{1,0:T(8,128)} copy(f32[1024,256]{1,0:T(8,128)S(1)} %get-tuple-element.4) | data formatting | bytes 2097152
  73.4 1.0 %copy.11 = f32[1024,256]{1,0:T(8,128)} copy(f32[1024,256]{1,0:T(8,128)S(1)} %get-tuple-element.5) | data formatting | bytes 2097152

commit v4 on v3

--- a/solution.py
+++ b/solution.py
@@ -164,19 +164,19 @@
     r_in, d_in, l_in, pl_in, j_in, pj_in,
     xs, rs,
     gd, gl, gj0, gj1, gn, gp, rv, pat_l, pat_j, ml, mj, mn,
-    left_d, left_dt, left_a, left_bt, left_x, left_j, left_e, left_r, left_m, left_g, left_n,
-    right_rl, right_lt, right_f, right_b, right_x, right_p, right_q, right_g, right_u, right_c, right_e,
-    u, xl, gt, pt, ga, pa, gg, ct, cn, w0, x0, wb, xb, ht, en, c_in, e_in, c_out, e_out,
-    send_sem, recv_sem, local_sem,
+    left_d, left_dt, left_a, left_bt, left_x, left_j, left_e, left_r, left_m, left_g, left_w,
+    right_rl, right_lt, right_f, right_b, right_x, right_p, right_q, right_g, right_u, right_c, right_e, right_n, right_xc, right_xe,
+    u, xl, pt, pa, ct, cn, x0, xb, et, xlt, gt, ga, w0, wb, ht, c_in, e_in, c_out, e_out,
+    send_sem, recv_sem, local_sem, ready_sem,
 ):
     rhs, node = lax.axis_index("rhs"), lax.axis_index("node")
     x, zl, y = rhs // 8, (rhs // 4) % 2, rhs % 4
-    after, before = lax.rem(node + 1, NODES), lax.rem(node + NODES - 1, NODES)
-    first = node == 0
+    after, before = node + 1, node - 1
+    first, last = node == 0, node == NODES - 1
     chip, odd = node // 2, node % 2 == 1
     even = jnp.logical_not(odd)
     partner = node + 1 - 2 * (node % 2)
-    two_after, two_before = lax.rem(node + 2, NODES), lax.rem(node + NODES - 2, NODES)
+    two_after, two_before = node + 2, node - 2
 
     def device(px, pz, py):
         return (px * 8 + pz * 4 + py, node)
@@ -192,10 +192,25 @@
     peers = [device(x, 1 - zl, y)]
     peers += [device(x, zl, lax.rem(y + k, 4)) for k in (1, 3)]
     peers += [device(lax.rem(x + k, 4), zl, y) for k in (1, 3)]
-    peers += [(rhs, to) for to in (after, before, two_after, two_before)]
     for peer in peers:
         pl.semaphore_signal(barrier, inc=1, device_id=peer, device_id_type=MESH_ID)
-    pl.semaphore_wait(barrier, len(peers))
+    for step in (1, 2):
+
+        @pl.when(node + step < NODES)
+        def _():
+            pl.semaphore_signal(barrier, inc=1, device_id=(rhs, node + step), device_id_type=MESH_ID)
+
+    for least in (0, 1, 2):
+
+        @pl.when(node == least if least < 2 else node >= 2)
+        def _():
+            pl.semaphore_wait(barrier, len(peers) + least)
+
+    for step in (1, 2):
+
+        @pl.when(node >= step)
+        def _():
+            pl.semaphore_signal(ready_sem.at[step - 1], inc=1, device_id=(rhs, node - step), device_id_type=MESH_ID)
 
     gathers = [
         Gather(sems, gd, x, zl, y, device, True),
@@ -256,8 +271,21 @@
     for q in (0, 1):
         for g in gathers:
             g.second.finish(q)
-    for copy in border[:2]:
-        copy.start()
+
+    @pl.when(node > 0)
+    def _():
+        border[0].start()
+        border[1].start()
+
+    @pl.when(last)
+    def _():
+        mn[...] = jnp.zeros_like(mn)
+        gn[...] = jnp.zeros_like(gn)
+
+    @pl.when(first)
+    def _():
+        gp[...] = jnp.zeros_like(gp)
+
 
     for g in later:
         g.start()
@@ -287,18 +315,22 @@
         put_right(right_f.at[s], fs)
         put_right(right_f.at[s], both[:, W:], W)
         if s == 3:
-            gt[...] = fs.T
+            gt[...] = fs.T.reshape(CHUNKS, PART, W)
             pt[...] = both[:, W:].T
 
     chunks = [slice(PART * k, PART * (k + 1)) for k in range(CHUNKS)]
-    down, fan_down, up, fan_up = [[sems.pair() for k in range(CHUNKS)] for _ in range(4)]
+    down, fan_down, up, fan_up, join, turn = [[sems.pair() for k in range(CHUNKS)] for _ in range(6)]
     hand = [
-        remote(gt, ga, sems.pair(), partner),
         remote(pt, pa, sems.pair(), partner),
-        remote(w0, wb, sems.pair(), partner),
         remote(x0, xb, sems.pair(), partner),
     ]
 
+    def send_g(k):
+        return remote(gt.at[k], ga.at[k], join[k], partner)
+
+    def send_w(k):
+        return remote(w0.at[k], wb.at[k], turn[k], partner)
+
     def send_down(k):
         return remote(c_out.at[k], c_in.at[k], down[k], two_after)
 
@@ -311,39 +343,66 @@
     def share_up(k):
         return remote(e_in.at[k], e_in.at[k], fan_up[k], partner)
 
+    for step in (1, 2):
+
+        @pl.when(node + step < NODES)
+        def _():
+            pl.semaphore_wait(ready_sem.at[step - 1], 1)
+
     @pl.when(even)
     def _():
+        for k in range(CHUNKS):
+            send_g(k).start()
         hand[0].start()
-        hand[1].start()
 
     @pl.when(chip == 0)
     def _():
         c_in[...] = jnp.zeros_like(c_in)
         left_m[...] = jnp.zeros_like(left_m)
 
-    @pl.when(chip == 3)
-    def _():
-        e_in[...] = jnp.zeros_like(e_in)
-
     @pl.when(odd)
     def _():
         put_right(right_p, pt[...])
+        for k, rows in enumerate(chunks):
+            send_g(k).wait_recv()
+            put_left(left_w.at[rows], ga[k])
+            c_out[k] = gt[k] + dot(left_w[rows, :], right_p[...])
+
+            @pl.when(chip == 0)
+            def _():
+                send_down(k).start()
+
         hand[0].wait_recv()
-        put_left(left_g, ga[...])
-        gg[...] = gt[...] + dot(left_g[...], right_p[...])
-
-    @pl.when(odd & (chip == 0))
-    def _():
-        for k, rows in enumerate(chunks):
-            c_out[k] = gg[rows, :]
-            send_down(k).start()
-
-    @pl.when(odd)
-    def _():
-        hand[1].wait_recv()
         put_left(left_g, pa[...])
         put_right(right_g, pa[...])
         put_right(right_q, dot(left_g[...], right_p[...]))
+
+    def turn_odd(k):
+        rows = chunks[k]
+        mine = ga[k] + dot(left_m[rows, :], right_g[...])
+        ct[rows, :] = mine
+        put_left(left_w.at[rows], mine)
+        w0[k] = xlt[rows, :] + dot(left_w[rows, :], right_xc[...])
+        send_w(k).start()
+
+    def turn_even(k):
+        rows = chunks[k]
+
+        @pl.when(chip > 0)
+        def _():
+            share_down(k).wait_recv()
+
+        ct[rows, :] = c_in[k]
+        put_left(left_m.at[rows], c_in[k])
+        mine = xlt[rows, :] + dot(left_m[rows, :], right_xc[...])
+        send_w(k).wait_recv()
+        put_left(left_w.at[rows], wb[k])
+        ht[k] = mine + dot(left_w[rows, :], right_xe[...])
+
+        @pl.when(chip == 3)
+        def _():
+            e_out[k] = ht[k]
+            send_up(k).start()
 
     def relay_down():
         for k, rows in enumerate(chunks):
@@ -352,10 +411,11 @@
 
             @pl.when(chip < 3)
             def _():
-                c_out[k] = gg[rows, :] + dot(left_m[rows, :], right_q[...])
+                c_out[k] = c_out[k] + dot(left_m[rows, :], right_q[...])
                 send_down(k).start()
 
             share_down(k).start()
+            pl.when(chip == 3)(lambda: turn_odd(k))
 
     for s in range(3):
         put_left(left_bt.at[s], -dot(left_dt[s], right_lt[s]))
@@ -367,6 +427,9 @@
             put_right(right_b, both)
         xl[s] = both[:, :W]
         put_left(left_x.at[s], both[:, W:])
+        if s == 0:
+            xlt[...] = both[:, :W].T
+            put_right(right_xc, both[:, W:].T)
 
     for g in later:
         g.crossed()
@@ -380,8 +443,11 @@
             g.first.finish(q)
             g.second.direct(q)
 
-    for copy in border[:2]:
-        copy.wait_recv()
+    @pl.when(jnp.logical_not(last))
+    def _():
+        border[0].wait_recv()
+        border[1].wait_recv()
+
     nxt = masked_panel(gn, None, lambda k: mn[k : k + 1, :])
     put_right(right_lt.at[3], nxt.T)
     for s in range(3, -1, -1):
@@ -392,52 +458,35 @@
         put_right(right_x, xe, W, 3 * W * (s + 1))
         put_left(left_x.at[s], xe, 3 * W)
         if s == 0:
-            x0[...] = xe
+            x0[...] = xe.T
 
     @pl.when(odd)
     def _():
-        hand[3].start()
+        hand[1].start()
 
     @pl.when(even)
     def _():
-        hand[3].wait_recv()
-        put_left(left_n, xb[...])
-        put_right(right_b, xb[...])
-        both = dot(left_x[0, :, 3 * W :], right_b[:, :W])
-        put_right(right_u, both.T)
+        put_right(right_xe, x0[...])
+        hand[1].wait_recv()
+        put_left(left_g, xb[...])
+        put_right(right_n, xb[...])
+        put_right(right_u, dot(left_g[...], right_xe[...]))
 
     pl.when(odd & (chip > 1))(relay_down)
 
-    @pl.when(odd)
-    def _():
-        ct[...] = ga[...] + dot(left_m[...], right_g[...])
-
-    @pl.when(even & (chip > 0))
+    @pl.when(odd & (chip < 3))
     def _():
         for k in range(CHUNKS):
-            share_down(k).wait_recv()
+            turn_odd(k)
 
     @pl.when(even)
     def _():
-        ct[...] = c_in[...].reshape(W, W)
-
-    cn[...] = ct[...].T
-    put_right(right_c, cn[...])
-    xl[0] = xl[0] + dot(left_x[0, :, : 3 * W], right_c[...])
-
-    @pl.when(odd)
-    def _():
-        w0[...] = xl[0]
-        hand[2].start()
-
-    border[2].start()
-
-    @pl.when(even)
-    def _():
-        hand[2].wait_recv()
-        put_right(right_b, wb[...])
-        both = dot(left_x[0, :, 3 * W :], right_b[:, :W])
-        ht[...] = (xl[0] + both).T
+        for k in range(CHUNKS):
+            turn_even(k)
+
+    @pl.when(jnp.logical_not(last))
+    def _():
+        border[2].start()
 
     def forward_later():
         for q in (0, 1):
@@ -445,14 +494,15 @@
                 g.second.forward(q)
 
     def prepare():
+        cn[...] = ct[...].T
+        put_right(right_c, cn[...])
         for s in range(4):
-            if s > 0:
-                xl[s] = xl[s] + dot(left_x[s, :, : 3 * W], right_c[...])
+            xl[s] = xl[s] + dot(left_x[s, :, : 3 * W], right_c[...])
             put_right(right_x, xl[s], 0, 3 * W * (s + 1))
         diagonal = lax.broadcasted_iota(jnp.int32, (W, W), 0) == lax.broadcasted_iota(jnp.int32, (W, W), 1)
         put_right(right_x, jnp.zeros((W, W), jnp.float32), 0, 15 * W)
         put_right(right_x, diagonal.astype(jnp.float32), W, 15 * W)
-        border[2].wait_recv()
+        pl.when(node > 0)(lambda: border[2].wait_recv())
         prev = jnp.concatenate(panel(gp, None), axis=0)
         put_left(left_e.at[1], prev.T)
         both = dot(left_e[0], right_x[3 * W : 6 * W, :])
@@ -475,40 +525,38 @@
     pl.when(chip < 3)(forward_later)
     pl.when(chip < 2)(prepare)
 
-    @pl.when(even)
+    @pl.when(even & (chip < 3))
     def _():
         for k, rows in enumerate(chunks):
-
-            @pl.when(chip < 3)
-            def _():
-                send_up(k).wait_recv()
+            send_up(k).wait_recv()
+            put_left(left_m.at[rows], e_in[k])
 
             @pl.when(chip > 0)
             def _():
-                put_left(left_m.at[rows], e_in[k])
-                e_out[k] = ht[rows, :] + dot(left_m[rows, :], right_u[...])
+                e_out[k] = ht[k] + dot(left_m[rows, :], right_u[...])
                 send_up(k).start()
 
-            @pl.when(chip < 3)
-            def _():
-                share_up(k).start()
+            share_up(k).start()
+            et[rows, :] = wb[k] + dot(left_m[rows, :], right_n[...])
+
+    @pl.when(even & (chip == 3))
+    def _():
+        et[...] = wb[...].reshape(W, W)
 
     pl.when(chip == 3)(forward_later)
     pl.when(chip > 1)(prepare)
 
     @pl.when(odd & (chip < 3))
     def _():
-        for k in range(CHUNKS):
+        for k, rows in enumerate(chunks):
             share_up(k).wait_recv()
-
-    en[...] = e_in[...].reshape(W, W).T
-
-    @pl.when(even)
-    def _():
-        put_right(right_b, en[...])
-        en[...] = wb[...] + dot(left_n[...], right_b[:, :W])
-
-    put_right(right_e, en[...])
+            et[rows, :] = e_in[k]
+
+    @pl.when(last)
+    def _():
+        et[...] = jnp.zeros_like(et)
+
+    put_right(right_e, et[...].T)
     for s in range(4):
         rows = slice(W * s, W * (s + 1))
         xs[rows, :] = xl[s] + dot(left_x[s, :, 3 * W :], right_e[...])
@@ -516,8 +564,15 @@
 
     for g in gathers + later:
         g.sent()
-    for copy in border:
-        copy.wait_send()
+
+    @pl.when(node > 0)
+    def _():
+        border[0].wait_send()
+        border[1].wait_send()
+
+    @pl.when(jnp.logical_not(last))
+    def _():
+        border[2].wait_send()
 
     def sent(cond, *copies):
         @pl.when(cond)
@@ -530,16 +585,16 @@
     sent(odd & (chip > 0), share_down)
     sent(even & (chip > 0), send_up)
     sent(even & (chip < 3), share_up)
+    sent(even, send_g)
+    sent(odd, send_w)
 
     @pl.when(even)
     def _():
         hand[0].wait_send()
+
+    @pl.when(odd)
+    def _():
         hand[1].wait_send()
-
-    @pl.when(odd)
-    def _():
-        hand[2].wait_send()
-        hand[3].wait_send()
 
 
 def on_device(*args):
@@ -587,6 +642,9 @@
             vmem((3 * W, W), bf16),
             vmem((3 * W, W), bf16),
             vmem((3 * W, W), bf16),
+            vmem((3 * W, W), bf16),
+            vmem((3 * W, W), bf16),
+            vmem((3 * W, W), bf16),
             vmem((4, W, W), f32),
             vmem((4, W, W), f32),
             vmem((W, W), f32),
@@ -597,18 +655,19 @@
             vmem((W, W), f32),
             vmem((W, W), f32),
             vmem((W, W), f32),
-            vmem((W, W), f32),
-            vmem((W, W), f32),
-            vmem((W, W), f32),
-            vmem((W, W), f32),
-            vmem((W, W), f32),
-            vmem((CHUNKS, PART, W), f32),
-            vmem((CHUNKS, PART, W), f32),
-            vmem((CHUNKS, PART, W), f32),
-            vmem((CHUNKS, PART, W), f32),
-            pltpu.SemaphoreType.DMA((76,)),
-            pltpu.SemaphoreType.DMA((76,)),
+            vmem((CHUNKS, PART, W), f32),
+            vmem((CHUNKS, PART, W), f32),
+            vmem((CHUNKS, PART, W), f32),
+            vmem((CHUNKS, PART, W), f32),
+            vmem((CHUNKS, PART, W), f32),
+            vmem((CHUNKS, PART, W), f32),
+            vmem((CHUNKS, PART, W), f32),
+            vmem((CHUNKS, PART, W), f32),
+            vmem((CHUNKS, PART, W), f32),
+            pltpu.SemaphoreType.DMA((84,)),
+            pltpu.SemaphoreType.DMA((84,)),
             pltpu.SemaphoreType.DMA((24,)),
+            pltpu.SemaphoreType.REGULAR((2,)),
         ],
         compiler_params=pltpu.CompilerParams(
             collective_id=0, has_side_effects=True, vmem_limit_bytes=48 * 1024 * 1024

time: 74.5 us -> 72.3 us (0.970)
  the two profiles are of different devices: /device:TPU:33 before, /device:TPU:1 now
where the time goes in v4:
time: 72.3 us; the launch traced here: 71.7 us
  Pallas kernels  69.1 us (96%)
  local copies, waits for them, and re-layouts  1.94 us (3%)
    pallas_call x1, Pallas kernels, on_device(): pl.pallas_call(kernel, out_shape=(out, out), in_specs=[hbm] * 6, out_spec...  69.1 us
    unnamed x2, local copies, waits for them, and re-layouts  1.94 us

profile of v4, /device:TPU:1, one launch (start us, length us, event | category | flops | bytes accessed | tf_op | source)
XLA Modules:
  0.0 71.7 jit_solution(3780403039836483069)
XLA Ops:
  0.6 69.1 %shard_map.77 = (f32[1024,256]{1,0:T(8,128)S(1)}, f32[1024,256]{1,0:T(8,128)S(1)}) custom-call(f32[1024,256]{1,0:T(8,128)} %r_in.1, f32[4,8,256]{2,1,0:T(8,128)} %d_in.1, f32[4,8,256]{2,1,0:T(8,128)} %l_in.1, s32[4,4,4]{2,1,0:T(4,128)} %pl_in.1, f32[4,8,768]{2,1,0:T(8,128)} %j_in.1, s32[4,4,12]{2,1,0:T(4,128)} %pj_in.1), custom_call_target="tpu_custom_call" | custom-call | tf_op jit(solution)/shard_map/pallas_call | solution.py:605
  69.8 1.0 %copy.10 = f32[1024,256]{1,0:T(8,128)} copy(f32[1024,256]{1,0:T(8,128)S(1)} %get-tuple-element.4) | data formatting | bytes 2097152
  70.7 1.0 %copy.11 = f32[1024,256]{1,0:T(8,128)} copy(f32[1024,256]{1,0:T(8,128)S(1)} %get-tuple-element.5) | data formatting | bytes 2097152

commit v5 on v4

--- a/solution.py
+++ b/solution.py
@@ -30,10 +30,11 @@
 
 
 class Ring:
-    def __init__(self, sems, where, pos, device_at):
-        self.where, self.pos = where, pos
+    def __init__(self, sems, where, pos, device_at, near=False):
+        self.where, self.pos, self.near = where, pos, near
+        self.opposite = device_at(lax.rem(pos + 2, 4))
         self.up, self.down = device_at(lax.rem(pos + 1, 4)), device_at(lax.rem(pos + 3, 4))
-        self.sems = {key: sems.pair() for key in ("u0", "d0", "u1", "d1", "fu", "fd")}
+        self.sems = {key: sems.pair() for key in ("u0", "d0", "u1", "d1", "f0", "f1")}
         self.started = {}
 
     def at(self, q, step):
@@ -56,25 +57,33 @@
         self.copy(key, *args).start()
 
     def direct(self, q, source=None):
-        first, second = ("u", "d") if q == 0 else ("d", "u")
+        if self.near and q == 1:
+            self.go("f1", 1, 0, self.opposite, source)
+        first, second = ("d", "u") if (q == 0) == self.near else ("u", "d")
         for way in (first, second):
             self.go(f"{way}{q}", q, 0, self.up if way == "u" else self.down, source)
 
+    def arrived(self, key, q, step):
+        self.copy(key, q, step, self.up).wait_recv()
+
     def forward(self, q):
-        if q == 0:
-            self.copy("u0", 0, 3, self.up).wait_recv()
-            self.go("fu", 0, 3, self.up)
+        if self.near:
+            if q == 0:
+                self.arrived("d0", 0, 1)
+                self.go("f0", 0, 1, self.down)
+        elif q == 0:
+            self.arrived("u0", 0, 3)
+            self.go("f0", 0, 3, self.up)
         else:
-            self.copy("d1", 1, 1, self.down).wait_recv()
-            self.go("fd", 1, 1, self.down)
+            self.arrived("d1", 1, 1)
+            self.go("f1", 1, 1, self.down)
 
     def finish(self, q):
-        if q == 0:
-            self.copy("d0", 0, 1, self.down).wait_recv()
-            self.copy("fu", 0, 2, self.up).wait_recv()
-        else:
-            self.copy("u1", 1, 3, self.up).wait_recv()
-            self.copy("fd", 1, 2, self.down).wait_recv()
+        if self.near or q == 1:
+            self.arrived(f"u{q}", q, 3)
+        if (self.near and q == 1) or (not self.near and q == 0):
+            self.arrived(f"d{q}", q, 1)
+        self.arrived(f"f{q}", q, 2)
 
     def sent(self):
         for key, args in self.started.items():
@@ -89,10 +98,10 @@
             return zl if q == 0 else 1 - zl
 
         if y_first:
-            self.first = Ring(sems, lambda q, p: buf.at[x, layer(q), p], y, lambda p: device(x, zl, p))
+            self.first = Ring(sems, lambda q, p: buf.at[x, layer(q), p], y, lambda p: device(x, zl, p), True)
             self.second = Ring(sems, lambda q, p: buf.at[p, layer(q)], x, lambda p: device(p, zl, y))
         else:
-            self.first = Ring(sems, lambda q, p: buf.at[p, layer(q), y], x, lambda p: device(p, zl, y))
+            self.first = Ring(sems, lambda q, p: buf.at[p, layer(q), y], x, lambda p: device(p, zl, y), True)
             self.second = Ring(sems, lambda q, p: buf.at[:, layer(q), p], y, lambda p: device(x, zl, p))
         send, recv = sems.pair()
         self.cross_sems = send, recv
@@ -164,9 +173,9 @@
     r_in, d_in, l_in, pl_in, j_in, pj_in,
     xs, rs,
     gd, gl, gj0, gj1, gn, gp, rv, pat_l, pat_j, ml, mj, mn,
-    left_d, left_dt, left_a, left_bt, left_x, left_j, left_e, left_r, left_m, left_g, left_w,
-    right_rl, right_lt, right_f, right_b, right_x, right_p, right_q, right_g, right_u, right_c, right_e, right_n, right_xc, right_xe,
-    u, xl, pt, pa, ct, cn, x0, xb, et, xlt, gt, ga, w0, wb, ht, c_in, e_in, c_out, e_out,
+    left_d, left_dt, left_a, left_bt, left_x, left_j, left_e, left_r, left_m, left_g, left_w, left_v,
+    right_rl, right_lt, right_f, right_b, right_x, right_p, right_q, right_g, right_u, right_c, right_e, right_n, right_xc, right_xe, right_xca,
+    u, xl, pt, pa, ct, cn, x0, xea, et, xlt, xct, xla, xca, gt, ga, wb, ht, c_in, e_in, c_out, e_out, ea_out,
     send_sem, recv_sem, local_sem, ready_sem,
 ):
     rhs, node = lax.axis_index("rhs"), lax.axis_index("node")
@@ -190,8 +199,8 @@
 
     barrier = pltpu.get_barrier_semaphore()
     peers = [device(x, 1 - zl, y)]
-    peers += [device(x, zl, lax.rem(y + k, 4)) for k in (1, 3)]
-    peers += [device(lax.rem(x + k, 4), zl, y) for k in (1, 3)]
+    peers += [device(x, zl, lax.rem(y + k, 4)) for k in (1, 2, 3)]
+    peers += [device(lax.rem(x + k, 4), zl, y) for k in (1, 2, 3)]
     for peer in peers:
         pl.semaphore_signal(barrier, inc=1, device_id=peer, device_id_type=MESH_ID)
     for step in (1, 2):
@@ -319,18 +328,17 @@
             pt[...] = both[:, W:].T
 
     chunks = [slice(PART * k, PART * (k + 1)) for k in range(CHUNKS)]
-    down, fan_down, up, fan_up, join, turn = [[sems.pair() for k in range(CHUNKS)] for _ in range(6)]
+    down, fan_down, up, fan_up, join = [[sems.pair() for k in range(CHUNKS)] for _ in range(5)]
     hand = [
         remote(pt, pa, sems.pair(), partner),
-        remote(x0, xb, sems.pair(), partner),
+        remote(xlt, xla, sems.pair(), partner),
+        remote(xct, xca, sems.pair(), partner),
+        remote(x0, xea, sems.pair(), partner),
     ]
 
     def send_g(k):
         return remote(gt.at[k], ga.at[k], join[k], partner)
 
-    def send_w(k):
-        return remote(w0.at[k], wb.at[k], turn[k], partner)
-
     def send_down(k):
         return remote(c_out.at[k], c_in.at[k], down[k], two_after)
 
@@ -341,7 +349,7 @@
         return remote(e_out.at[k], e_in.at[k], up[k], two_before)
 
     def share_up(k):
-        return remote(e_in.at[k], e_in.at[k], fan_up[k], partner)
+        return remote(ea_out.at[k], e_in.at[k], fan_up[k], partner)
 
     for step in (1, 2):
 
@@ -377,32 +385,25 @@
         put_right(right_g, pa[...])
         put_right(right_q, dot(left_g[...], right_p[...]))
 
-    def turn_odd(k):
+    def turn(k):
         rows = chunks[k]
         mine = ga[k] + dot(left_m[rows, :], right_g[...])
         ct[rows, :] = mine
         put_left(left_w.at[rows], mine)
-        w0[k] = xlt[rows, :] + dot(left_w[rows, :], right_xc[...])
-        send_w(k).start()
-
-    def turn_even(k):
-        rows = chunks[k]
-
-        @pl.when(chip > 0)
+        wb[k] = xlt[rows, :] + dot(left_w[rows, :], right_xc[...])
+        put_left(left_v.at[rows], wb[k])
+        head = xla[rows, :] + dot(left_m[rows, :], right_xca[...]) + dot(left_v[rows, :], right_xe[...])
+
+        @pl.when(chip < 3)
         def _():
-            share_down(k).wait_recv()
-
-        ct[rows, :] = c_in[k]
-        put_left(left_m.at[rows], c_in[k])
-        mine = xlt[rows, :] + dot(left_m[rows, :], right_xc[...])
-        send_w(k).wait_recv()
-        put_left(left_w.at[rows], wb[k])
-        ht[k] = mine + dot(left_w[rows, :], right_xe[...])
+            ht[k] = head
 
         @pl.when(chip == 3)
         def _():
-            e_out[k] = ht[k]
+            e_out[k] = head
             send_up(k).start()
+            ea_out[k] = wb[k]
+            share_up(k).start()
 
     def relay_down():
         for k, rows in enumerate(chunks):
@@ -415,7 +416,7 @@
                 send_down(k).start()
 
             share_down(k).start()
-            pl.when(chip == 3)(lambda: turn_odd(k))
+            pl.when(chip == 3)(lambda: turn(k))
 
     for s in range(3):
         put_left(left_bt.at[s], -dot(left_dt[s], right_lt[s]))
@@ -429,11 +430,20 @@
         put_left(left_x.at[s], both[:, W:])
         if s == 0:
             xlt[...] = both[:, :W].T
-            put_right(right_xc, both[:, W:].T)
+            xct[...] = both[:, W:].T
+
+    @pl.when(even)
+    def _():
+        hand[1].start()
+        hand[2].start()
+
+    @pl.when(odd)
+    def _():
+        put_right(right_xc, xct[...])
 
     for g in later:
         g.crossed()
-    pl.when(odd & (chip == 1))(relay_down)
+    pl.when(odd & (chip > 0) & (chip < 3))(relay_down)
 
     for q in (0, 1):
         for g in later:
@@ -460,29 +470,36 @@
         if s == 0:
             x0[...] = xe.T
 
+    @pl.when(even)
+    def _():
+        hand[3].start()
+
     @pl.when(odd)
     def _():
-        hand[1].start()
+        put_right(right_n, x0[...])
+        put_left(left_g, x0[...])
+        hand[1].wait_recv()
+        hand[2].wait_recv()
+        put_right(right_xca, xca[...])
+        hand[3].wait_recv()
+        put_right(right_xe, xea[...])
+        put_right(right_u, dot(left_g[...], right_xe[...]))
+
+    pl.when(odd & (chip == 3))(relay_down)
+
+    @pl.when(odd & (chip < 3))
+    def _():
+        for k in range(CHUNKS):
+            turn(k)
 
     @pl.when(even)
     def _():
-        put_right(right_xe, x0[...])
-        hand[1].wait_recv()
-        put_left(left_g, xb[...])
-        put_right(right_n, xb[...])
-        put_right(right_u, dot(left_g[...], right_xe[...]))
-
-    pl.when(odd & (chip > 1))(relay_down)
-
-    @pl.when(odd & (chip < 3))
-    def _():
-        for k in range(CHUNKS):
-            turn_odd(k)
-
-    @pl.when(even)
-    def _():
-        for k in range(CHUNKS):
-            turn_even(k)
+        @pl.when(chip > 0)
+        def _():
+            for k in range(CHUNKS):
+                share_down(k).wait_recv()
+
+        ct[...] = c_in[...].reshape(W, W)
 
     @pl.when(jnp.logical_not(last))
     def _():
@@ -522,41 +539,36 @@
             rs[W * s : W * (s + 1), :] = rv[W * s : W * (s + 1), :] - both[:, :W]
             put_left(left_r.at[s], -both[:, W:])
 
-    pl.when(chip < 3)(forward_later)
-    pl.when(chip < 2)(prepare)
-
-    @pl.when(even & (chip < 3))
+    pl.when(even | (chip < 3))(forward_later)
+    pl.when(even | (chip == 0))(prepare)
+
+    @pl.when(odd & (chip < 3))
     def _():
         for k, rows in enumerate(chunks):
             send_up(k).wait_recv()
-            put_left(left_m.at[rows], e_in[k])
+            put_left(left_v.at[rows], e_in[k])
 
             @pl.when(chip > 0)
             def _():
-                e_out[k] = ht[k] + dot(left_m[rows, :], right_u[...])
+                e_out[k] = ht[k] + dot(left_v[rows, :], right_u[...])
                 send_up(k).start()
 
+            ea_out[k] = wb[k] + dot(left_v[rows, :], right_n[...])
             share_up(k).start()
-            et[rows, :] = wb[k] + dot(left_m[rows, :], right_n[...])
-
-    @pl.when(even & (chip == 3))
-    def _():
-        et[...] = wb[...].reshape(W, W)
-
-    pl.when(chip == 3)(forward_later)
-    pl.when(chip > 1)(prepare)
-
-    @pl.when(odd & (chip < 3))
-    def _():
-        for k, rows in enumerate(chunks):
+
+    pl.when(odd & (chip == 3))(forward_later)
+    pl.when(odd & (chip > 0))(prepare)
+
+    @pl.when(even)
+    def _():
+        for k in range(CHUNKS):
             share_up(k).wait_recv()
-            et[rows, :] = e_in[k]
 
     @pl.when(last)
     def _():
-        et[...] = jnp.zeros_like(et)
-
-    put_right(right_e, et[...].T)
+        e_in[...] = jnp.zeros_like(e_in)
+
+    put_right(right_e, e_in[...].reshape(W, W).T)
     for s in range(4):
         rows = slice(W * s, W * (s + 1))
         xs[rows, :] = xl[s] + dot(left_x[s, :, 3 * W :], right_e[...])
@@ -583,18 +595,14 @@
 
     sent(odd & (chip < 3), send_down)
     sent(odd & (chip > 0), share_down)
-    sent(even & (chip > 0), send_up)
-    sent(even & (chip < 3), share_up)
+    sent(odd & (chip > 0), send_up)
+    sent(odd, share_up)
     sent(even, send_g)
-    sent(odd, send_w)
 
     @pl.when(even)
     def _():
-        hand[0].wait_send()
-
-    @pl.when(odd)
-    def _():
-        hand[1].wait_send()
+        for copy in hand:
+            copy.wait_send()
 
 
 def on_device(*args):
@@ -631,6 +639,7 @@
             vmem((W, 3 * W), bf16),
             vmem((W, 3 * W), bf16),
             vmem((W, 3 * W), bf16),
+            vmem((W, 3 * W), bf16),
             vmem((4, 3 * W, 2 * W), bf16),
             vmem((4, 3 * W, W), bf16),
             vmem((4, 3 * W, 2 * W), bf16),
@@ -645,8 +654,12 @@
             vmem((3 * W, W), bf16),
             vmem((3 * W, W), bf16),
             vmem((3 * W, W), bf16),
+            vmem((3 * W, W), bf16),
             vmem((4, W, W), f32),
             vmem((4, W, W), f32),
+            vmem((W, W), f32),
+            vmem((W, W), f32),
+            vmem((W, W), f32),
             vmem((W, W), f32),
             vmem((W, W), f32),
             vmem((W, W), f32),

time: 72.3 us -> 71.3 us (0.986)
  no operation moved by 1% of the time
where the time goes in v5:
time: 71.3 us; the launch traced here: 71.2 us
  Pallas kernels  68.6 us (96%)
  local copies, waits for them, and re-layouts  1.94 us (3%)
    pallas_call x1, Pallas kernels, on_device(): pl.pallas_call(kernel, out_shape=(out, out), in_specs=[hbm] * 6, out_spec...  68.6 us
    unnamed x2, local copies, waits for them, and re-layouts  1.94 us

profile of v5, /device:TPU:1, one launch (start us, length us, event | category | flops | bytes accessed | tf_op | source)
XLA Modules:
  0.0 71.2 jit_solution(9621785052831654586)
XLA Ops:
  0.6 68.6 %shard_map.77 = (f32[1024,256]{1,0:T(8,128)S(1)}, f32[1024,256]{1,0:T(8,128)S(1)}) custom-call(f32[1024,256]{1,0:T(8,128)} %r_in.1, f32[4,8,256]{2,1,0:T(8,128)} %d_in.1, f32[4,8,256]{2,1,0:T(8,128)} %l_in.1, s32[4,4,4]{2,1,0:T(4,128)} %pl_in.1, f32[4,8,768]{2,1,0:T(8,128)} %j_in.1, s32[4,4,12]{2,1,0:T(4,128)} %pj_in.1), custom_call_target="tpu_custom_call" | custom-call | tf_op jit(solution)/shard_map/pallas_call | solution.py:613
  69.2 1.0 %copy.10 = f32[1024,256]{1,0:T(8,128)} copy(f32[1024,256]{1,0:T(8,128)S(1)} %get-tuple-element.4) | data formatting | bytes 2097152
  70.2 1.0 %copy.11 = f32[1024,256]{1,0:T(8,128)} copy(f32[1024,256]{1,0:T(8,128)S(1)} %get-tuple-element.5) | data formatting | bytes 2097152

commit v6 on v5

--- a/solution.py
+++ b/solution.py
@@ -274,9 +274,31 @@
         ml[s] = rows_of(pat_l[s])
         for c in range(3):
             mj[s, :, W * c : W * (c + 1)] = rows_of(pat_j[s, :, 4 * c : 4 * (c + 1)])
+    def stage(number):
+        def run():
+            if number < 2:
+                for g in later:
+                    (g.start, g.crossed)[number]()
+                return
+            for q in (0, 1):
+                for g in later:
+                    if number == 2:
+                        g.first.forward(q)
+                    elif number == 3:
+                        g.first.finish(q)
+                        g.second.direct(q)
+                    else:
+                        g.second.forward(q)
+
+        return run
+
+    early = chip > 1
+    slow = chip < 2
+    pl.when(early)(stage(0))
     for q in (0, 1):
         for g in gathers:
             g.second.forward(q)
+    pl.when(early)(stage(1))
     for q in (0, 1):
         for g in gathers:
             g.second.finish(q)
@@ -296,8 +318,8 @@
         gp[...] = jnp.zeros_like(gp)
 
 
-    for g in later:
-        g.start()
+    pl.when(slow)(stage(0))
+    pl.when(early)(stage(2))
 
     for s in range(4):
         d = jnp.concatenate(panel(gd, s), axis=0)
@@ -368,6 +390,13 @@
         c_in[...] = jnp.zeros_like(c_in)
         left_m[...] = jnp.zeros_like(left_m)
 
+    @pl.when(slow)
+    def _():
+        stage(1)()
+        stage(2)()
+
+    pl.when(early)(stage(3))
+
     @pl.when(odd)
     def _():
         put_right(right_p, pt[...])
@@ -418,6 +447,7 @@
             share_down(k).start()
             pl.when(chip == 3)(lambda: turn(k))
 
+    pl.when(odd & (chip == 0))(stage(3))
     for s in range(3):
         put_left(left_bt.at[s], -dot(left_dt[s], right_lt[s]))
     for s in range(3, -1, -1):
@@ -441,17 +471,9 @@
     def _():
         put_right(right_xc, xct[...])
 
-    for g in later:
-        g.crossed()
     pl.when(odd & (chip > 0) & (chip < 3))(relay_down)
 
-    for q in (0, 1):
-        for g in later:
-            g.first.forward(q)
-    for q in (0, 1):
-        for g in later:
-            g.first.finish(q)
-            g.second.direct(q)
+    pl.when((even & slow) | (node == 3))(stage(3))
 
     @pl.when(jnp.logical_not(last))
     def _():
@@ -485,6 +507,7 @@
         put_right(right_xe, xea[...])
         put_right(right_u, dot(left_g[...], right_xe[...]))
 
+    pl.when(odd & (chip == 3))(stage(4))
     pl.when(odd & (chip == 3))(relay_down)
 
     @pl.when(odd & (chip < 3))
@@ -504,11 +527,6 @@
     @pl.when(jnp.logical_not(last))
     def _():
         border[2].start()
-
-    def forward_later():
-        for q in (0, 1):
-            for g in later:
-                g.second.forward(q)
 
     def prepare():
         cn[...] = ct[...].T
@@ -539,7 +557,7 @@
             rs[W * s : W * (s + 1), :] = rv[W * s : W * (s + 1), :] - both[:, :W]
             put_left(left_r.at[s], -both[:, W:])
 
-    pl.when(even | (chip < 3))(forward_later)
+    pl.when(even | (chip < 3))(stage(4))
     pl.when(even | (chip == 0))(prepare)
 
     @pl.when(odd & (chip < 3))
@@ -556,7 +574,6 @@
             ea_out[k] = wb[k] + dot(left_v[rows, :], right_n[...])
             share_up(k).start()
 
-    pl.when(odd & (chip == 3))(forward_later)
     pl.when(odd & (chip > 0))(prepare)
 
     @pl.when(even)

time: 71.3 us -> 66.7 us (0.935)
  Pallas kernels: 68.6 us -> 64 us
    pallas_call x1, Pallas kernels: 68.6 us -> 64 us  [on_device(): pl.pallas_call(kernel, out_shape=(out, out), in_specs=[hbm] * 6, out_spec...]
where the time goes in v6:
time: 66.7 us; the launch traced here: 66.6 us
  Pallas kernels  64 us (96%)
  local copies, waits for them, and re-layouts  1.94 us (3%)
    pallas_call x1, Pallas kernels, on_device(): pl.pallas_call(kernel, out_shape=(out, out), in_specs=[hbm] * 6, out_spec...  64 us
    unnamed x2, local copies, waits for them, and re-layouts  1.94 us

profile of v6, /device:TPU:1, one launch (start us, length us, event | category | flops | bytes accessed | tf_op | source)
XLA Modules:
  0.0 66.6 jit_solution(9525226038331319004)
XLA Ops:
  0.6 64.0 %shard_map.77 = (f32[1024,256]{1,0:T(8,128)S(1)}, f32[1024,256]{1,0:T(8,128)S(1)}) custom-call(f32[1024,256]{1,0:T(8,128)} %r_in.1, f32[4,8,256]{2,1,0:T(8,128)} %d_in.1, f32[4,8,256]{2,1,0:T(8,128)} %l_in.1, s32[4,4,4]{2,1,0:T(4,128)} %pl_in.1, f32[4,8,768]{2,1,0:T(8,128)} %j_in.1, s32[4,4,12]{2,1,0:T(4,128)} %pj_in.1), custom_call_target="tpu_custom_call" | custom-call | tf_op jit(solution)/shard_map/pallas_call | solution.py:630
  64.6 1.0 %copy.10 = f32[1024,256]{1,0:T(8,128)} copy(f32[1024,256]{1,0:T(8,128)S(1)} %get-tuple-element.4) | data formatting | bytes 2097152
  65.6 1.0 %copy.11 = f32[1024,256]{1,0:T(8,128)} copy(f32[1024,256]{1,0:T(8,128)S(1)} %get-tuple-element.5) | data formatting | bytes 2097152

commit v7 on v6

--- a/solution.py
+++ b/solution.py
@@ -171,11 +171,11 @@
 
 def kernel(
     r_in, d_in, l_in, pl_in, j_in, pj_in,
-    xs, rs,
+    xl, rs, left_x, left_r, right_e,
     gd, gl, gj0, gj1, gn, gp, rv, pat_l, pat_j, ml, mj, mn,
-    left_d, left_dt, left_a, left_bt, left_x, left_j, left_e, left_r, left_m, left_g, left_w, left_v,
-    right_rl, right_lt, right_f, right_b, right_x, right_p, right_q, right_g, right_u, right_c, right_e, right_n, right_xc, right_xe, right_xca,
-    u, xl, pt, pa, ct, cn, x0, xea, et, xlt, xct, xla, xca, gt, ga, wb, ht, c_in, e_in, c_out, e_out, ea_out,
+    left_d, left_dt, left_a, left_bt, left_c, left_j, left_e, left_m, left_g, left_w, left_v,
+    right_rl, right_lt, right_f, right_b, right_x, right_p, right_q, right_g, right_u, right_c, right_n, right_xc, right_xe, right_xca,
+    u, pt, pa, ct, cn, x0, xea, et, xlt, xct, xla, xca, gt, ga, wb, ht, c_in, e_in, c_out, e_out, ea_out,
     send_sem, recv_sem, local_sem, ready_sem,
 ):
     rhs, node = lax.axis_index("rhs"), lax.axis_index("node")
@@ -263,10 +263,16 @@
     for q in (0, 1):
         for g in gathers:
             g.first.forward(q)
+    def second_pieces():
+        for g in gathers:
+            g.second.direct(1)
+
     for q in (0, 1):
         for g in gathers:
             g.first.finish(q)
-            g.second.direct(q)
+            if q == 0:
+                g.second.direct(0)
+    pl.when(even)(second_pieces)
     r_load.wait()
     for copy in pat_loads + j_loads:
         copy.wait()
@@ -295,9 +301,11 @@
     early = chip > 1
     slow = chip < 2
     pl.when(early)(stage(0))
-    for q in (0, 1):
-        for g in gathers:
-            g.second.forward(q)
+    for g in gathers:
+        g.second.forward(0)
+    pl.when(odd)(second_pieces)
+    for g in gathers:
+        g.second.forward(1)
     pl.when(early)(stage(1))
     for q in (0, 1):
         for g in gathers:
@@ -324,15 +332,10 @@
     for s in range(4):
         d = jnp.concatenate(panel(gd, s), axis=0)
         put_left(left_d.at[s], d)
-        put_left(left_dt.at[s], d.T)
         low = masked_panel(gl, s, lambda k: ml[s, k : k + 1, :])
         right = right_rl.at[s]
         put_right(right, rv[W * s : W * (s + 1), :])
         put_right(right, low, W)
-        if s == 0:
-            put_left(left_e.at[0], -low.T)
-        else:
-            put_right(right_lt.at[s - 1], low.T)
         both = dot(left_d[s], right[...])
         if s == 0:
             put_right(right_f.at[0], both[:, :W])
@@ -448,6 +451,13 @@
             pl.when(chip == 3)(lambda: turn(k))
 
     pl.when(odd & (chip == 0))(stage(3))
+    for s in range(4):
+        put_left(left_dt.at[s], jnp.concatenate(panel(gd, s), axis=0).T)
+        low = masked_panel(gl, s, lambda k: ml[s, k : k + 1, :])
+        if s == 0:
+            put_left(left_e.at[0], -low.T)
+        else:
+            put_right(right_lt.at[s - 1], low.T)
     for s in range(3):
         put_left(left_bt.at[s], -dot(left_dt[s], right_lt[s]))
     for s in range(3, -1, -1):
@@ -457,7 +467,7 @@
         if s > 0:
             put_right(right_b, both)
         xl[s] = both[:, :W]
-        put_left(left_x.at[s], both[:, W:])
+        put_left(left_c.at[s], both[:, W:])
         if s == 0:
             xlt[...] = both[:, :W].T
             xct[...] = both[:, W:].T
@@ -488,7 +498,7 @@
         else:
             xe = dot(left_bt[s], right_x[3 * W * (s + 2) : 3 * W * (s + 3), W:])
         put_right(right_x, xe, W, 3 * W * (s + 1))
-        put_left(left_x.at[s], xe, 3 * W)
+        put_left(left_x.at[s], xe)
         if s == 0:
             x0[...] = xe.T
 
@@ -532,7 +542,7 @@
         cn[...] = ct[...].T
         put_right(right_c, cn[...])
         for s in range(4):
-            xl[s] = xl[s] + dot(left_x[s, :, : 3 * W], right_c[...])
+            xl[s] = xl[s] + dot(left_c[s], right_c[...])
             put_right(right_x, xl[s], 0, 3 * W * (s + 1))
         diagonal = lax.broadcasted_iota(jnp.int32, (W, W), 0) == lax.broadcasted_iota(jnp.int32, (W, W), 1)
         put_right(right_x, jnp.zeros((W, W), jnp.float32), 0, 15 * W)
@@ -586,11 +596,6 @@
         e_in[...] = jnp.zeros_like(e_in)
 
     put_right(right_e, e_in[...].reshape(W, W).T)
-    for s in range(4):
-        rows = slice(W * s, W * (s + 1))
-        xs[rows, :] = xl[s] + dot(left_x[s, :, 3 * W :], right_e[...])
-        rs[rows, :] = rs[rows, :] + dot(left_r[s], right_e[...])
-
     for g in gathers + later:
         g.sent()
 
@@ -622,16 +627,35 @@
             copy.wait_send()
 
 
+def last_kernel(xl, rs, left_x, left_r, right_e, sol_out, res_out, buf, sem):
+    copies = []
+    for s in range(4):
+        rows = slice(W * s, W * (s + 1))
+        for k, (base, left, out) in enumerate(((xl[s], left_x, sol_out), (rs[rows, :], left_r, res_out))):
+            buf[k, rows, :] = base + dot(left[s], right_e[...])
+            copies.append(pltpu.make_async_copy(buf.at[k, rows], out.at[rows], sem.at[k, s]))
+            copies[-1].start()
+    for copy in copies:
+        copy.wait()
+
+
 def on_device(*args):
     f32, bf16 = jnp.float32, jnp.bfloat16
-    out = jax.ShapeDtypeStruct(args[0].shape, f32)
-    hbm = pl.BlockSpec(memory_space=pltpu.HBM)
-    vmem = pltpu.VMEM
-    return pl.pallas_call(
+    rows, columns = args[0].shape
+    hbm, vmem = pl.BlockSpec(memory_space=pltpu.HBM), pltpu.VMEM
+    held = pl.BlockSpec(memory_space=vmem)
+    shape = jax.ShapeDtypeStruct
+    parts = pl.pallas_call(
         kernel,
-        out_shape=(out, out),
+        out_shape=(
+            shape((4, W, W), f32),
+            shape((4 * W, W), f32),
+            shape((4, W, 3 * W), bf16),
+            shape((4, W, 3 * W), bf16),
+            shape((3 * W, W), bf16),
+        ),
         in_specs=[hbm] * 6,
-        out_specs=(pl.BlockSpec(memory_space=vmem),) * 2,
+        out_specs=(held,) * 5,
         scratch_shapes=[
             vmem((4, 2, 4, 4, 8, W), f32),
             vmem((4, 2, 4, 4, 8, W), f32),
@@ -649,10 +673,9 @@
             vmem((4, W, 3 * W), bf16),
             vmem((4, W, 3 * W), bf16),
             vmem((3, W, 3 * W), bf16),
-            vmem((4, W, 6 * W), bf16),
+            vmem((4, W, 3 * W), bf16),
             vmem((W, 9 * W), bf16),
             vmem((2, W, 3 * W), bf16),
-            vmem((4, W, 3 * W), bf16),
             vmem((W, 3 * W), bf16),
             vmem((W, 3 * W), bf16),
             vmem((W, 3 * W), bf16),
@@ -671,8 +694,6 @@
             vmem((3 * W, W), bf16),
             vmem((3 * W, W), bf16),
             vmem((3 * W, W), bf16),
-            vmem((3 * W, W), bf16),
-            vmem((4, W, W), f32),
             vmem((4, W, W), f32),
             vmem((W, W), f32),
             vmem((W, W), f32),
@@ -703,6 +724,15 @@
             collective_id=0, has_side_effects=True, vmem_limit_bytes=48 * 1024 * 1024
         ),
     )(*[pltpu.with_memory_space_constraint(a, pltpu.HBM) for a in args])
+    out = shape((rows, columns), f32)
+    return pl.pallas_call(
+        last_kernel,
+        out_shape=(out, out),
+        in_specs=[held] * 5,
+        out_specs=(hbm, hbm),
+        scratch_shapes=[vmem((2, rows, columns), f32), pltpu.SemaphoreType.DMA((2, 4))],
+        compiler_params=pltpu.CompilerParams(vmem_limit_bytes=16 * 1024 * 1024),
+    )(*parts)
 
 
 def solution(mesh):

time: 66.7 us -> 66.9 us (level)
  the two profiles are of different devices: /device:TPU:1 before, /device:TPU:3 now
where the time goes in v7:
time: 66.9 us; the launch traced here: 66.8 us
  Pallas kernels  66 us (99%)
  between operations  0.8 us (1%)
    pallas_call x1, Pallas kernels, on_device(): pl.pallas_call(kernel, out_shape=(shape((4, W, W), f32), shape((4 * W, W)...  64.1 us
    pallas_call x1, Pallas kernels, on_device(): pl.pallas_call(last_kernel, out_shape=(out, out), in_specs=[held] * 5, ou...  1.91 us

profile of v7, /device:TPU:3, one launch (start us, length us, event | category | flops | bytes accessed | tf_op | source)
XLA Modules:
  0.0 66.8 jit_solution(7026894072579497161)
XLA Ops:
  0.6 64.1 %shard_map.77 = (f32[4,256,256]{2,1,0:T(8,128)S(1)}, f32[1024,256]{1,0:T(8,128)S(1)}, bf16[4,256,768]{2,1,0:T(8,128)(2,1)S(1)}, bf16[4,256,768]{2,1,0:T(8,128)(2,1)S(1)}, bf16[768,256]{1,0:T(8,128)(2,1)S(1)}) custom-call(f32[1024,256]{1,0:T(8,128)} %r_in.1, f32[4,8,256]{2,1,0:T(8,128)} %d_in.1, f32[4,8,256]{2,1,0:T(8,128)} %l_in.1, s32[4,4,4]{2,1,0:T(4,128)} %pl_in.1, ...), custom_call_target="tpu_custom_call" | custom-call | tf_op jit(solution)/shard_map/pallas_call | solution.py:648
  64.7 1.9 %shard_map.78 = (f32[1024,256]{1,0:T(8,128)}, f32[1024,256]{1,0:T(8,128)}) custom-call(f32[4,256,256]{2,1,0:T(8,128)S(1)} %get-tuple-element.7.xl, f32[1024,256]{1,0:T(8,128)S(1)} %get-tuple-element.8.rs, bf16[4,256,768]{2,1,0:T(8,128)(2,1)S(1)} %get-tuple-element.9.left_x, bf16[4,256,768]{2,1,0:T(8,128)(2,1)S(1)} %get-tuple-element.10.left_r, ...), custom_call_target="tpu_custom_call" | custom-call | tf_op jit(solution)/shard_map/pallas_call | solution.py:728

commit v8 on v7

--- a/solution.py
+++ b/solution.py
@@ -9,7 +9,7 @@
 B = 64
 W = 256
 NODES = 8
-CHUNKS = 4
+CHUNKS = 8
 PART = W // CHUNKS
 
 
@@ -426,16 +426,10 @@
         put_left(left_v.at[rows], wb[k])
         head = xla[rows, :] + dot(left_m[rows, :], right_xca[...]) + dot(left_v[rows, :], right_xe[...])
 
-        @pl.when(chip < 3)
-        def _():
-            ht[k] = head
-
-        @pl.when(chip == 3)
-        def _():
-            e_out[k] = head
-            send_up(k).start()
-            ea_out[k] = wb[k]
-            share_up(k).start()
+        e_out[k] = head
+        send_up(k).start()
+        ea_out[k] = wb[k]
+        share_up(k).start()
 
     def relay_down():
         for k, rows in enumerate(chunks):
@@ -450,7 +444,7 @@
             share_down(k).start()
             pl.when(chip == 3)(lambda: turn(k))
 
-    pl.when(odd & (chip == 0))(stage(3))
+    pl.when(chip == 0)(stage(3))
     for s in range(4):
         put_left(left_dt.at[s], jnp.concatenate(panel(gd, s), axis=0).T)
         low = masked_panel(gl, s, lambda k: ml[s, k : k + 1, :])
@@ -483,7 +477,7 @@
 
     pl.when(odd & (chip > 0) & (chip < 3))(relay_down)
 
-    pl.when((even & slow) | (node == 3))(stage(3))
+    pl.when(chip == 1)(stage(3))
 
     @pl.when(jnp.logical_not(last))
     def _():
@@ -522,8 +516,14 @@
 
     @pl.when(odd & (chip < 3))
     def _():
-        for k in range(CHUNKS):
-            turn(k)
+        mine = ga[...].reshape(W, W) + dot(left_m[...], right_g[...])
+        ct[...] = mine
+        put_left(left_w, mine)
+        mine = xlt[...] + dot(left_w[...], right_xc[...])
+        wb[...] = mine.reshape(CHUNKS, PART, W)
+        put_left(left_v, mine)
+        head = xla[...] + dot(left_m[...], right_xca[...]) + dot(left_v[...], right_xe[...])
+        ht[...] = head.reshape(CHUNKS, PART, W)
 
     @pl.when(even)
     def _():
@@ -715,8 +715,8 @@
             vmem((CHUNKS, PART, W), f32),
             vmem((CHUNKS, PART, W), f32),
             vmem((CHUNKS, PART, W), f32),
-            pltpu.SemaphoreType.DMA((84,)),
-            pltpu.SemaphoreType.DMA((84,)),
+            pltpu.SemaphoreType.DMA((104,)),
+            pltpu.SemaphoreType.DMA((104,)),
             pltpu.SemaphoreType.DMA((24,)),
             pltpu.SemaphoreType.REGULAR((2,)),
         ],

time: 66.9 us -> 66.3 us (level)
  the two profiles are of different devices: /device:TPU:3 before, /device:TPU:1 now
where the time goes in v8:
time: 66.3 us; the launch traced here: 66.2 us
  Pallas kernels  65.4 us (99%)
  between operations  0.8 us (1%)
    pallas_call x1, Pallas kernels, on_device(): pl.pallas_call(kernel, out_shape=(shape((4, W, W), f32), shape((4 * W, W)...  63.5 us
    pallas_call x1, Pallas kernels, on_device(): pl.pallas_call(last_kernel, out_shape=(out, out), in_specs=[held] * 5, ou...  1.91 us

profile of v8, /device:TPU:1, one launch (start us, length us, event | category | flops | bytes accessed | tf_op | source)
XLA Modules:
  0.0 66.2 jit_solution(9108279225661312001)
XLA Ops:
  0.6 63.5 %shard_map.77 = (f32[4,256,256]{2,1,0:T(8,128)S(1)}, f32[1024,256]{1,0:T(8,128)S(1)}, bf16[4,256,768]{2,1,0:T(8,128)(2,1)S(1)}, bf16[4,256,768]{2,1,0:T(8,128)(2,1)S(1)}, bf16[768,256]{1,0:T(8,128)(2,1)S(1)}) custom-call(f32[1024,256]{1,0:T(8,128)} %r_in.1, f32[4,8,256]{2,1,0:T(8,128)} %d_in.1, f32[4,8,256]{2,1,0:T(8,128)} %l_in.1, s32[4,4,4]{2,1,0:T(4,128)} %pl_in.1, ...), custom_call_target="tpu_custom_call" | custom-call | tf_op jit(solution)/shard_map/pallas_call | solution.py:648
  64.1 1.9 %shard_map.78 = (f32[1024,256]{1,0:T(8,128)}, f32[1024,256]{1,0:T(8,128)}) custom-call(f32[4,256,256]{2,1,0:T(8,128)S(1)} %get-tuple-element.7.xl, f32[1024,256]{1,0:T(8,128)S(1)} %get-tuple-element.8.rs, bf16[4,256,768]{2,1,0:T(8,128)(2,1)S(1)} %get-tuple-element.9.left_x, bf16[4,256,768]{2,1,0:T(8,128)(2,1)S(1)} %get-tuple-element.10.left_r, ...), custom_call_target="tpu_custom_call" | custom-call | tf_op jit(solution)/shard_map/pallas_call | solution.py:728

commit v9 on v8

--- a/solution.py
+++ b/solution.py
@@ -197,6 +197,7 @@
         copy.start()
         return copy
 
+    owns = [load(d_in, gd.at[x, zl, y]), load(l_in, gl.at[x, zl, y])]
     barrier = pltpu.get_barrier_semaphore()
     peers = [device(x, 1 - zl, y)]
     peers += [device(x, zl, lax.rem(y + k, 4)) for k in (1, 2, 3)]
@@ -240,15 +241,14 @@
             device_id_type=MESH_ID,
         )
 
-    for g, source in zip(gathers, (d_in, l_in)):
-        g.start(source)
+    for g, own in zip(gathers, owns):
+        own.wait()
+        g.start()
     border = [
         remote(ml.at[0], mn, sems.pair(), before),
         remote(gl.at[:, :, :, 0], gn, sems.pair(), before),
         remote(gd.at[:, :, :, 3], gp, sems.pair(), after),
     ]
-    own_d = load(d_in, gd.at[x, zl, y])
-    own_l = load(l_in, gl.at[x, zl, y])
     pat_loads = [load(pl_in, pat_l), load(pj_in, pat_j)]
     j_loads = []
     for h, gj in enumerate((gj0, gj1)):
@@ -256,8 +256,6 @@
             for c in range(3):
                 j_loads.append(load(j_in.at[2 * h + s, :, W * c : W * (c + 1)], gj.at[x, zl, y, 3 * s + c]))
     r_load = load(r_in, rv)
-    own_d.wait()
-    own_l.wait()
     for g in gathers:
         g.crossed()
     for q in (0, 1):

time: 66.3 us -> 65.1 us (0.982)
  Pallas kernels: 65.4 us -> 64.2 us
    pallas_call x1, Pallas kernels: 63.5 us -> 62.3 us  [on_device(): pl.pallas_call(kernel, out_shape=(shape((4, W, W), f32), shape((4 * W, W)...]
where the time goes in v9:
time: 65.1 us; the launch traced here: 65 us
  Pallas kernels  64.2 us (99%)
  between operations  0.8 us (1%)
    pallas_call x1, Pallas kernels, on_device(): pl.pallas_call(kernel, out_shape=(shape((4, W, W), f32), shape((4 * W, W)...  62.3 us
    pallas_call x1, Pallas kernels, on_device(): pl.pallas_call(last_kernel, out_shape=(out, out), in_specs=[held] * 5, ou...  1.91 us

profile of v9, /device:TPU:1, one launch (start us, length us, event | category | flops | bytes accessed | tf_op | source)
XLA Modules:
  0.0 65.0 jit_solution(12860388410987257906)
XLA Ops:
  0.6 62.3 %shard_map.77 = (f32[4,256,256]{2,1,0:T(8,128)S(1)}, f32[1024,256]{1,0:T(8,128)S(1)}, bf16[4,256,768]{2,1,0:T(8,128)(2,1)S(1)}, bf16[4,256,768]{2,1,0:T(8,128)(2,1)S(1)}, bf16[768,256]{1,0:T(8,128)(2,1)S(1)}) custom-call(f32[1024,256]{1,0:T(8,128)} %r_in.1, f32[4,8,256]{2,1,0:T(8,128)} %d_in.1, f32[4,8,256]{2,1,0:T(8,128)} %l_in.1, s32[4,4,4]{2,1,0:T(4,128)} %pl_in.1, ...), custom_call_target="tpu_custom_call" | custom-call | tf_op jit(solution)/shard_map/pallas_call | solution.py:646
  62.9 1.9 %shard_map.78 = (f32[1024,256]{1,0:T(8,128)}, f32[1024,256]{1,0:T(8,128)}) custom-call(f32[4,256,256]{2,1,0:T(8,128)S(1)} %get-tuple-element.7.xl, f32[1024,256]{1,0:T(8,128)S(1)} %get-tuple-element.8.rs, bf16[4,256,768]{2,1,0:T(8,128)(2,1)S(1)} %get-tuple-element.9.left_x, bf16[4,256,768]{2,1,0:T(8,128)(2,1)S(1)} %get-tuple-element.10.left_r, ...), custom_call_target="tpu_custom_call" | custom-call | tf_op jit(solution)/shard_map/pallas_call | solution.py:726
